TPU v7x, 256 devices: a whole 4x4x8 slice. The times are simulated.
256 devices in a mesh: region: 8 (over x, core), patch: 32 (over y, z).
Axes of the slice: x: 4, y: 4, z: 8, core: 2. Of those that a mesh axis runs over, the one named last changes fastest.
Arguments:
- nodes: bfloat16 [65536, 512], P(('region', 'patch')), may hold values from -6 to 6
- edges: bfloat16 [262144, 512], P(('region', 'patch')), may hold values from -6 to 6
- node_cotan: bfloat16 [65536, 512], P(('region', 'patch')), may hold values from -6 to 6
- edge_cotan: bfloat16 [262144, 512], P(('region', 'patch')), may hold values from -6 to 6
- edge_inner: bfloat16 [1536, 512], replicated, may hold values from -0.15625 to 0.15625
- edge_outer: bfloat16 [512, 512], replicated, may hold values from -0.25 to 0.25
- node_inner: bfloat16 [1024, 512], replicated, may hold values from -0.1875 to 0.1875
- node_outer: bfloat16 [512, 512], replicated, may hold values from -0.25 to 0.25
- edge_shift: float32 [512], replicated, may hold values from -4 to 4
- edge_offset: float32 [512], replicated, may hold values from -4 to 4
- edge_gain: float32 [512], replicated, may hold values from 0.5 to 1.5
- node_shift: float32 [512], replicated, may hold values from -4 to 4
- node_offset: float32 [512], replicated, may hold values from -4 to 4
- node_gain: float32 [512], replicated, may hold values from 0.5 to 1.5
- send_rows: int32 [8, 32, 2, 32], P('region', 'patch'), may hold values from -1 to 255, as said below
- senders: int32 [262144], P(('region', 'patch')), may hold values from 0 to 319, as said below
- receivers: int32 [262144], P(('region', 'patch')), may hold values from 0 to 255
Outputs:
- grad_nodes: float32 [65536, 512], P(('region', 'patch'))
- grad_edges: bfloat16 [262144, 512], P(('region', 'patch'))
- grad_weights: float32 [1835008], P(('region', 'patch'))
- grad_vectors: float32 [3072], replicated
Inputs may be any that keep to these rules, and one draw needn't show every extreme that they name: `send_rows`: list 0 of a patch goes to the patch one index below, list 1 to the one above, cyclically within its region. Live entries are distinct own-node indices and stand first, the rest are -1; each list has half of 32 to 32 live entries, and some list is full. `senders`: below 256 a sender is an own node; 256 + j is the j-th row received from the patch below, 288 + j the j-th from the patch above; only live rows are named.
All inputs are finite; a program needn't handle non-finite values.
Results may differ from a plain program's by a relative error of at most 0.0063.
Values may be sent and summed in bfloat16 or wider, within the bound.
A program may use at most 128 MiB of HBM per device.

v0:
```python
import math

import jax
import jax.numpy as jnp
from jax import lax
from jax.sharding import PartitionSpec as P


def extended(block, sides, width):
    for axis, dim in sides:
        count = lax.axis_size(axis)
        forward = [(i, i + 1) for i in range(count - 1)]
        forward.append((count - 1, 0))
        backward = [(target, source) for source, target in forward]
        low = lax.ppermute(
            lax.slice_in_dim(block, block.shape[dim] - width, None, axis=dim), axis, forward
        )
        high = lax.ppermute(lax.slice_in_dim(block, 0, width, axis=dim), axis, backward)
        block = jnp.concatenate([low, block, high], axis=dim)
    return block


def layer_norm(values):
    centred = values - jnp.mean(values, axis=-1, keepdims=True)
    invstd = lax.rsqrt(jnp.mean(centred * centred, axis=-1, keepdims=True) + 1e-05)
    return (centred * invstd, invstd)


def norm_back(upstream, normed, invstd, gains):
    scaled = upstream * gains
    return invstd * (
        scaled
        - jnp.mean(scaled, axis=-1, keepdims=True)
        - normed * jnp.mean(scaled * normed, axis=-1, keepdims=True)
    )


def activation_grad(preact):
    sigmoid_val = jax.nn.sigmoid(preact)
    return sigmoid_val * (1.0 + preact * (1.0 - sigmoid_val))


def contract_rows(left, right):
    return lax.dot_general(
        left, right, (((0,), (0,)), ((), ())), preferred_element_type=jnp.float32
    )


def per_device(
    nodes,
    edges,
    node_cotan,
    edge_cotan,
    edge_inner,
    edge_outer,
    node_inner,
    node_outer,
    edge_shift,
    edge_offset,
    edge_gain,
    node_shift,
    node_offset,
    node_gain,
    send_rows,
    senders,
    receivers,
):
    node_count = nodes.shape[0]
    edge_count = edges.shape[0]
    feature_width = nodes.shape[1]
    send_lists = send_rows.reshape(-1)
    slot_count = send_lists.shape[0] // 2
    devices_all = lax.axis_size("region") * lax.axis_size("patch")
    edge_norm = 1.0 / math.sqrt(edge_count * devices_all)
    node_norm = 1.0 / math.sqrt(node_count * devices_all)
    node_ids = jnp.arange(node_count, dtype=jnp.int32)
    pick_send = (send_lists[:, None] == node_ids[None, :]).astype(jnp.bfloat16)
    outgoing = jnp.dot(pick_send, nodes, preferred_element_type=jnp.float32).astype(jnp.bfloat16)
    received = extended(outgoing.reshape(2, slot_count, feature_width), (("patch", 0),), 1)
    lookup = jnp.concatenate([nodes, received[0], received[3]], axis=0)
    lookup_ids = jnp.arange(lookup.shape[0], dtype=jnp.int32)
    pick_sender = (senders[:, None] == lookup_ids[None, :]).astype(jnp.bfloat16)
    pick_receiver = (receivers[:, None] == node_ids[None, :]).astype(jnp.bfloat16)
    sender_rows = jnp.dot(pick_sender, lookup, preferred_element_type=jnp.float32).astype(
        jnp.bfloat16
    )
    receiver_rows = jnp.dot(pick_receiver, nodes, preferred_element_type=jnp.float32).astype(
        jnp.bfloat16
    )
    edge_inputs = jnp.concatenate([edges, sender_rows, receiver_rows], axis=1)
    edge_preact = jnp.dot(edge_inputs, edge_inner, preferred_element_type=jnp.float32) + edge_shift
    edge_hidden = jax.nn.silu(edge_preact).astype(jnp.bfloat16)
    edge_linear = jnp.dot(edge_hidden, edge_outer, preferred_element_type=jnp.float32) + edge_offset
    edge_normed, edge_invstd = layer_norm(edge_linear)
    edge_fresh = (edges.astype(jnp.float32) + edge_gain * edge_normed).astype(jnp.bfloat16)
    aggregate = contract_rows(pick_receiver, edge_fresh).astype(jnp.bfloat16)
    node_inputs = jnp.concatenate([nodes, aggregate], axis=1)
    node_preact = jnp.dot(node_inputs, node_inner, preferred_element_type=jnp.float32) + node_shift
    node_hidden = jax.nn.silu(node_preact).astype(jnp.bfloat16)
    node_linear = jnp.dot(node_hidden, node_outer, preferred_element_type=jnp.float32) + node_offset
    node_normed, node_invstd = layer_norm(node_linear)
    cotan_node = node_cotan.astype(jnp.float32)
    linear_back = norm_back(cotan_node, node_normed, node_invstd, node_gain)
    linear_half = linear_back.astype(jnp.bfloat16)
    preact_back = jnp.dot(
        linear_half, node_outer.T, preferred_element_type=jnp.float32
    ) * activation_grad(node_preact)
    preact_half = preact_back.astype(jnp.bfloat16)
    inputs_back = jnp.dot(preact_half, node_inner.T, preferred_element_type=jnp.float32)
    aggregate_half = inputs_back[:, feature_width:].astype(jnp.bfloat16)
    fresh_back = edge_cotan.astype(jnp.float32) + jnp.dot(
        pick_receiver, aggregate_half, preferred_element_type=jnp.float32
    )
    elinear_back = norm_back(fresh_back, edge_normed, edge_invstd, edge_gain)
    elinear_half = elinear_back.astype(jnp.bfloat16)
    epreact_back = jnp.dot(
        elinear_half, edge_outer.T, preferred_element_type=jnp.float32
    ) * activation_grad(edge_preact)
    epreact_half = epreact_back.astype(jnp.bfloat16)
    einputs_back = jnp.dot(epreact_half, edge_inner.T, preferred_element_type=jnp.float32)
    grad_edges = (fresh_back + einputs_back[:, :feature_width]).astype(jnp.bfloat16)
    sender_half = einputs_back[:, feature_width : 2 * feature_width].astype(jnp.bfloat16)
    receiver_half = einputs_back[:, 2 * feature_width :].astype(jnp.bfloat16)
    lookup_back = contract_rows(pick_sender, sender_half)
    rim_back = lookup_back[node_count:].reshape(2, slot_count, feature_width)
    returned = extended(rim_back.astype(jnp.bfloat16), (("patch", 0),), 1).astype(rim_back.dtype)
    back_rows = jnp.concatenate([returned[0], returned[3]], axis=0)
    from_rims = lax.dot_general(
        pick_send.astype(jnp.float32),
        back_rows,
        (((0,), (0,)), ((), ())),
        precision=lax.Precision.HIGHEST,
        preferred_element_type=jnp.float32,
    )
    grad_nodes = (
        cotan_node
        + inputs_back[:, :feature_width]
        + lookup_back[:node_count]
        + contract_rows(pick_receiver, receiver_half)
        + from_rims
    )
    flat_terms = jnp.concatenate(
        [
            (contract_rows(edge_inputs, epreact_half) * edge_norm).reshape(-1),
            (contract_rows(edge_hidden, elinear_half) * edge_norm).reshape(-1),
            (contract_rows(node_inputs, preact_half) * node_norm).reshape(-1),
            (contract_rows(node_hidden, linear_half) * node_norm).reshape(-1),
        ]
    )
    vector_terms = jnp.concatenate(
        [
            jnp.sum(epreact_back, axis=0) * edge_norm,
            jnp.sum(elinear_back, axis=0) * edge_norm,
            jnp.sum(fresh_back * edge_normed, axis=0) * edge_norm,
            jnp.sum(preact_back, axis=0) * node_norm,
            jnp.sum(linear_back, axis=0) * node_norm,
            jnp.sum(cotan_node * node_normed, axis=0) * node_norm,
        ]
    )
    grad_vectors = lax.psum(vector_terms, ("region", "patch"))
    grad_weights = lax.psum_scatter(
        flat_terms, ("region", "patch"), scatter_dimension=0, tiled=True
    )
    return (grad_nodes, grad_edges, grad_weights, grad_vectors)


def solution(mesh):
    in_specs = (
        P(("region", "patch"), None),
        P(("region", "patch"), None),
        P(("region", "patch"), None),
        P(("region", "patch"), None),
        P(),
        P(),
        P(),
        P(),
        P(),
        P(),
        P(),
        P(),
        P(),
        P(),
        P("region", "patch", None, None),
        P(("region", "patch")),
        P(("region", "patch")),
    )
    out_specs = (
        P(("region", "patch"), None),
        P(("region", "patch"), None),
        P(("region", "patch")),
        P(),
    )
    return jax.shard_map(
        per_device, mesh=mesh, in_specs=in_specs, out_specs=out_specs, check_vma=False
    )
```

profile of v0, /device:TPU:2, one launch (start us, length us, event | category | flops | bytes accessed | tf_op | source)
XLA Modules:
  0.0 339.4 jit_solution(11202574372045446276)
XLA Ops:
  8.1 1.2 convolution_convert_fusion.2
  9.3 2.0 collective-permute-start
  11.3 6.5 %collective-permute-start.1 = (bf16[1,32,512]{2,1,0:T(8,128)(2,1)S(1)}, bf16[1,32,512]{2,1,0:T(8,128)(2,1)S(1)}, u32[]{:S(2)}, u32[]{:S(2)}) collective-permute-start(bf16[1,32,512]{2,1,0:T(8,128)(2,1)S(1)} %get-tuple-element.27), channel_id=1, source_target_pairs={{1,0},{2,1},{3,2},{4,3},{5,4},{6,5},{7,6},{8,7},{9,8},{10,9},{11,1... | collective-permute-start | bytes 98312 | tf_op jit(solution)/shard_map/ppermute | solution.py:18
  17.7 1.6 convolution_convert_fusion
  19.3 2.7 copy.27
  22.0 2.3 copy.29
  25.5 1.8 fusion.6
  29.0 1.0 convolution_convert_fusion.1
  34.5 1.3 multiply_reduce_fusion
  35.8 1.0 fusion.57
  37.1 1.3 fusion.61
  41.0 2.1 fusion
  45.0 10.8 %pad_maximum_fusion = f32[1835008]{0:T(1024)} fusion(f32[262144]{0:T(1024)S(1)} %bitcast.48, f32[524288]{0:T(1024)S(1)} %bitcast.46, f32[262144]{0:T(1024)S(1)} %bitcast.47, f32[786432]{0:T(1024)S(1)} %bitcast.45), kind=kLoop, calls=%fused_computation | loop fusion | flops 5505024 | bytes 14680064 | tf_op jit(solution)/shard_map/concatenate | solution.py:142
  55.8 3.5 %fusion.59 = (bf16[1024,1536]{1,0:T(8,128)(2,1)}, f32[1024,1536]{1,0:T(8,128)S(1)}) fusion(bf16[1536,512]{1,0:T(8,128)(2,1)S(1)} %copy-done, bf16[1024,512]{1,0:T(8,128)(2,1)S(1)} %get-tuple-element.38), kind=kOutput, calls=%fused_computation.117 | convolution fusion | flops 1612185600 | bytes 12058624 | tf_op jit(solution)/shard_map/dot_general | solution.py:120
  59.2 1.5 slice.84
  60.8 2.9 copy.34
  63.7 3.4 %fusion.60 = (bf16[320,512]{1,0:T(8,128)(2,1)S(1)}, f32[320,512]{1,0:T(8,128)}) fusion(bf16[1024,1536]{1,0:T(8,128)(2,1)} %get-tuple-element.33, s32[1024]{0:T(1024)S(1)} %copy-done.17), kind=kOutput, calls=%fused_computation.118 | convolution fusion | flops 336035840 | bytes 2035712 | tf_op jit(solution)/shard_map/dot_general | solution.py:44
  67.2 5.3 %collective-permute-start.3 = (bf16[1,32,512]{2,1,0:T(8,128)(2,1)S(1)}, bf16[1,32,512]{2,1,0:T(8,128)(2,1)S(1)}, u32[]{:S(2)}, u32[]{:S(2)}) collective-permute-start(bf16[1,32,512]{2,1,0:T(8,128)(2,1)S(1)} %get-tuple-element.23), channel_id=1, source_target_pairs={{1,0},{2,1},{3,2},{4,3},{5,4},{6,5},{7,6},{8,7},{9,8},{10,9},{11,1... | collective-permute-start | bytes 98312 | tf_op jit(solution)/shard_map/ppermute | solution.py:18
  72.6 1.9 add_convert_fusion
  74.5 1.3 copy.32
  75.8 72.9 %psum.7 = f32[3072]{0:T(1024)} all-reduce(f32[3072]{0:T(1024)S(1)} %constant_dynamic-update-slice_fusion), channel_id=1, replica_groups=mesh['region'=8,'patch'=32] {'region','patch'}, use_global_device_ids=true, to_apply=%region_15.16 | all-reduce | flops 3072 | bytes 24576 | tf_op jit(solution)/shard_map/psum | solution.py:160
  149.3 3.0 fusion.7
  152.3 178.8 %all-reduce.3.cloned.1.call-done = f32[1835008]{0:T(1024)} async-done(((f32[1835008]{0:T(1024)}), f32[1835008]{0:T(1024)}) %all-reduce.3.cloned.1.call-update) | async-done | bytes 7340048
  331.1 1.4 dynamic-slice
  (86 shorter events, 13.4 us)
Async XLA Ops:
  7.2 18.0 %copy-start = (bf16[1536,512]{1,0:T(8,128)(2,1)S(1)}, bf16[1536,512]{1,0:T(8,128)(2,1)}, u32[]{:S(2)}) copy-start(bf16[1536,512]{1,0:T(8,128)(2,1)} %param.21) | copy-start | bytes 4718596
  7.2 324.0 %all-reduce.3.cloned.1.call-start = ((), (), s32[]{:S(2)}) async-start(), calls=%async_computation | async-start | bytes 14680064
  9.3 15.0 %collective-permute-start = (bf16[1,32,512]{2,1,0:T(8,128)(2,1)S(1)}, bf16[1,32,512]{2,1,0:T(8,128)(2,1)S(1)}, u32[]{:S(2)}, u32[]{:S(2)}) collective-permute-start(bf16[1,32,512]{2,1,0:T(8,128)(2,1)S(1)} %get-tuple-element.26), channel_id=1, source_target_pairs={{0,1},{1,2},{2,3},{3,4},{4,5},{5,6},{6,7},{7,8},{8,9},{9,10},{10,1... | collective-permute-start | bytes 98312 | tf_op jit(solution)/shard_map/ppermute | solution.py:15
  11.3 13.0 %collective-permute-start.1 = (bf16[1,32,512]{2,1,0:T(8,128)(2,1)S(1)}, bf16[1,32,512]{2,1,0:T(8,128)(2,1)S(1)}, u32[]{:S(2)}, u32[]{:S(2)}) collective-permute-start(bf16[1,32,512]{2,1,0:T(8,128)(2,1)S(1)} %get-tuple-element.27), channel_id=1, source_target_pairs={{1,0},{2,1},{3,2},{4,3},{5,4},{6,5},{7,6},{8,7},{9,8},{10,9},{11,1... | collective-permute-start | bytes 98312 | tf_op jit(solution)/shard_map/ppermute | solution.py:18
  19.3 5.9 %copy-start.6 = (bf16[1024,512]{0,1:T(8,128)(2,1)}, bf16[1024,512]{0,1:T(8,128)(2,1)S(1)}, u32[]{:S(2)}) copy-start(bf16[1024,512]{0,1:T(8,128)(2,1)S(1)} %convolution_convert_fusion) | copy-start | bytes 3145732
  19.3 5.0 %copy-start.4 = (bf16[256,512]{1,0:T(8,128)(2,1)S(1)}, bf16[256,512]{1,0:T(8,128)(2,1)}, u32[]{:S(2)}) copy-start(bf16[256,512]{1,0:T(8,128)(2,1)} %param.17) | copy-start | bytes 786436
  19.3 5.0 %copy-start.17 = (s32[1024]{0:T(1024)S(1)}, s32[1024]{0:T(1024)}, u32[]{:S(2)}) copy-start(s32[1024]{0:T(1024)} %param.32) | copy-start | bytes 12292
  24.3 1.2 copy-start.9
  25.5 1.8 copy-start.13
  25.5 1.9 copy-start.16
  25.5 1.9 copy-start.20
  29.0 1.2 copy-start.8
  29.0 1.2 copy-start.18
  30.2 1.0 copy-start.15
  30.2 1.0 copy-start.19
  31.3 1.0 copy-start.5
  31.3 1.0 copy-start.12
  33.2 1.2 copy-start.10
  34.5 1.3 copy-start.3
  35.8 1.4 copy-start.1
  39.7 1.2 copy-start.7
  63.7 8.8 %copy-start.2 = (f32[1024,512]{0,1:T(8,128)S(1)}, f32[1024,512]{0,1:T(8,128)}, u32[]{:S(2)}) copy-start(f32[1024,512]{0,1:T(8,128)} %copy-done.1) | copy-start | bytes 6291460
  67.2 81.6 %collective-permute-start.2 = (bf16[1,32,512]{2,1,0:T(8,128)(2,1)S(1)}, bf16[1,32,512]{2,1,0:T(8,128)(2,1)S(1)}, u32[]{:S(2)}, u32[]{:S(2)}) collective-permute-start(bf16[1,32,512]{2,1,0:T(8,128)(2,1)S(1)} %get-tuple-element.22), channel_id=1, source_target_pairs={{0,1},{1,2},{2,3},{3,4},{4,5},{5,6},{6,7},{7,8},{8,9},{9,10},{10,1... | collective-permute-start | bytes 98312 | tf_op jit(solution)/shard_map/ppermute | solution.py:15
  67.2 81.6 %collective-permute-start.3 = (bf16[1,32,512]{2,1,0:T(8,128)(2,1)S(1)}, bf16[1,32,512]{2,1,0:T(8,128)(2,1)S(1)}, u32[]{:S(2)}, u32[]{:S(2)}) collective-permute-start(bf16[1,32,512]{2,1,0:T(8,128)(2,1)S(1)} %get-tuple-element.23), channel_id=1, source_target_pairs={{1,0},{2,1},{3,2},{4,3},{5,4},{6,5},{7,6},{8,7},{9,8},{10,9},{11,1... | collective-permute-start | bytes 98312 | tf_op jit(solution)/shard_map/ppermute | solution.py:18
  (2 other events, 1.4 us)
Sparse Core Ops, SparseCore 0:
  55.9 275.2 all-reduce.2
where the time goes:
time: 340 us; the launch traced here: 339 us
  waiting for transfers between devices  179 us (53%)
  blocking collectives  72.9 us (21%)
  matrix products  25.8 us (8%)
  local copies, waits for them, and re-layouts  18.5 us (5%)
  other arithmetic  14.9 us (4%)
  between operations  14.4 us (4%)
  starting transfers between devices  13.8 us (4%)
    unnamed x2, waiting for transfers between devices  179 us
    psum x1, blocking collectives, per_device(): grad_vectors = lax.psum(vector_terms, ('region', 'patch'))  72.9 us
    unnamed x51, local copies, waits for them, and re-layouts  16.1 us
    ppermute x2, starting transfers between devices, extended(): lax.ppermute(lax.slice_in_dim(block, 0, width, axis=dim), axis, backward)  11.8 us
    dot_general x7, matrix products, contract_rows(): lax.dot_general(left, right, (((0,), (0,)), ((), ())), preferred_element_...  11.1 us
    concatenate x1, other arithmetic, per_device(): jnp.concatenate([(contract_rows(edge_inputs, epreact_half) * edge_norm).r...  10.8 us
  transfers between devices with their start and end apart: 5, of which 1 were waited for; matrix products, arithmetic and copies ran while one was open for 7% of the time, Pallas kernels for 0%

commit v1 on v0

--- a/solution.py
+++ b/solution.py
@@ -3,7 +3,403 @@
 import jax
 import jax.numpy as jnp
 from jax import lax
+from jax.experimental import pallas as pl
+from jax.experimental.pallas import tpu as pltpu
 from jax.sharding import PartitionSpec as P
+
+MESH = pl.DeviceIdType.MESH
+NX, NC, NY, NZ = 4, 2, 4, 8
+WIDTH, HALF = 512, 256
+BLOCK, QUARTER, SHARE, PAD = 448, 112, 14, 16
+
+
+def coordinates():
+    region, patch = lax.axis_index("region"), lax.axis_index("patch")
+    return region // NC, lax.rem(region, NC), patch // NZ, lax.rem(patch, NZ)
+
+
+def at(x, c, y, z):
+    return (x * NC + c, y * NZ + z)
+
+
+def peers():
+    x, c, y, z = coordinates()
+    found = [at(x, 1 - c, y, z)]
+    found += [at(lax.rem(x + k, NX), c, y, z) for k in range(1, NX)]
+    found += [at(x, c, lax.rem(y + k, NY), z) for k in range(1, NY)]
+    found += [at(x, c, y, lax.rem(z + k, NZ)) for k in range(1, NZ)]
+    return found
+
+
+def entry_barrier():
+    barrier = pltpu.get_barrier_semaphore()
+    found = peers()
+    for device in found:
+        pl.semaphore_signal(barrier, inc=1, device_id=device, device_id_type=MESH)
+    pl.semaphore_wait(barrier, len(found))
+
+
+def send(src, dst, send_sem, recv_sem, device):
+    return pltpu.make_async_remote_copy(
+        src_ref=src,
+        dst_ref=dst,
+        send_sem=send_sem,
+        recv_sem=recv_sem,
+        device_id=device,
+        device_id_type=MESH,
+    )
+
+
+def chunks(total, step, body):
+    def one(i, carry):
+        body(pl.multiple_of(i * step, step))
+        return carry
+
+    lax.fori_loop(0, total // step, one, 0)
+
+
+def reduce_scratch():
+    bf16, f32 = jnp.bfloat16, jnp.float32
+    dma = pltpu.SemaphoreType.DMA
+    return dict(
+        sb=pltpu.VMEM((NX, NC, BLOCK, WIDTH), bf16),
+        r0=pltpu.VMEM((NX, BLOCK, WIDTH), bf16),
+        b1=pltpu.VMEM((NX, BLOCK, WIDTH), bf16),
+        r1x=pltpu.VMEM((NX, BLOCK, HALF), bf16),
+        r1y=pltpu.VMEM((NY, NX, QUARTER, HALF), bf16),
+        a1x=pltpu.VMEM((NY, QUARTER, HALF), f32),
+        b2x=pltpu.VMEM((NY, QUARTER, HALF), bf16),
+        r2x=pltpu.VMEM((NY, QUARTER, HALF), bf16),
+        a1y=pltpu.VMEM((NX, QUARTER, HALF), f32),
+        b2y=pltpu.VMEM((NX, QUARTER, HALF), bf16),
+        r2y=pltpu.VMEM((NX, QUARTER, HALF), bf16),
+        packed=pltpu.VMEM((NZ, PAD, WIDTH), f32),
+        b3=pltpu.VMEM((NZ, PAD, WIDTH), bf16),
+        r3=pltpu.VMEM((NZ, PAD, WIDTH), bf16),
+        s0=dma((NX,)),
+        q0=dma((NX,)),
+        s1x=dma((NX,)),
+        q1x=dma((NX,)),
+        s1y=dma((2, NY)),
+        q1y=dma((2, NY)),
+        s2x=dma((NY,)),
+        q2x=dma((NY,)),
+        s2y=dma((NX,)),
+        q2y=dma((NX,)),
+        s3=dma((NZ,)),
+        q3=dma((NZ,)),
+        vc=pltpu.VMEM((2, 8, WIDTH), f32),
+        vx=pltpu.VMEM((NX, 8, WIDTH), f32),
+        vy=pltpu.VMEM((NY, 8, WIDTH), f32),
+        vz=pltpu.VMEM((NZ, 8, WIDTH), f32),
+        us=dma((1 + NX + NY + NZ,)),
+        uq=dma((1 + NX + NY + NZ,)),
+    )
+
+
+class Reducer:
+    def __init__(self, g, bufs):
+        self.g, self.b = g, bufs
+        self.x, self.c, self.y, self.z = coordinates()
+        self.piece_xs = ((2, 3), (0, 1))
+
+    def core_copies(self, piece):
+        b = self.b
+        return [
+            send(
+                b["sb"].at[xx, 1 - self.c],
+                b["r0"].at[xx],
+                b["s0"].at[xx],
+                b["q0"].at[xx],
+                at(self.x, 1 - self.c, self.y, self.z),
+            )
+            for xx in self.piece_xs[piece]
+        ]
+
+    def core_start(self, piece):
+        for copy in self.core_copies(piece):
+            copy.start()
+
+    def round_blocks(self, piece):
+        b, g = self.b, self.g
+        for xx in self.piece_xs[piece]:
+            for cc in range(NC):
+
+                def body(i, xx=xx, cc=cc):
+                    b["sb"][xx, cc, pl.ds(i, 64)] = g[xx, cc, pl.ds(i, 64)].astype(jnp.bfloat16)
+
+                chunks(BLOCK, 64, body)
+
+    def first_x(self, xx):
+        b = self.b
+        return send(
+            b["b1"].at[xx, :, pl.ds(0, HALF)],
+            b["r1x"].at[self.x],
+            b["s1x"].at[xx],
+            b["q1x"].at[self.x],
+            at(xx, self.c, self.y, self.z),
+        )
+
+    def first_y(self, piece, k):
+        b = self.b
+        to = lax.rem(self.y + k, NY)
+        xa = self.piece_xs[piece][0]
+        return send(
+            b["b1"].at[pl.ds(xa, 2), pl.ds(pl.multiple_of(to * QUARTER, 16), QUARTER), pl.ds(HALF, HALF)],
+            b["r1y"].at[k, pl.ds(xa, 2)],
+            b["s1y"].at[piece, k],
+            b["q1y"].at[piece, k],
+            at(self.x, self.c, to, self.z),
+        )
+
+    def first_start(self, piece):
+        b, g = self.b, self.g
+        for copy in self.core_copies(piece):
+            copy.wait_recv()
+        for xx in self.piece_xs[piece]:
+
+            def body(i, xx=xx):
+                total = g[xx, self.c, pl.ds(i, 64)] + b["r0"][xx, pl.ds(i, 64)].astype(jnp.float32)
+                g[xx, self.c, pl.ds(i, 64)] = total
+                b["b1"][xx, pl.ds(i, 64)] = total.astype(jnp.bfloat16)
+
+            chunks(BLOCK, 64, body)
+        for k in (2, 1, 3):
+            self.first_y(piece, k).start()
+        for xx in self.piece_xs[piece]:
+
+            @pl.when(self.x != xx)
+            def _(xx=xx):
+                self.first_x(xx).start()
+
+    def second_x(self, k):
+        b = self.b
+        to = lax.rem(self.y + k, NY)
+        return send(
+            b["b2x"].at[to],
+            b["r2x"].at[k],
+            b["s2x"].at[k],
+            b["q2x"].at[k],
+            at(self.x, self.c, to, self.z),
+        )
+
+    def second_y(self, xx):
+        b = self.b
+        return send(
+            b["b2y"].at[xx],
+            b["r2y"].at[self.x],
+            b["s2y"].at[xx],
+            b["q2y"].at[self.x],
+            at(xx, self.c, self.y, self.z),
+        )
+
+    def second_y_start(self, piece):
+        b, g = self.b, self.g
+        for k in (1, 3, 2):
+            self.first_y(piece, k).wait_recv()
+        base = self.y * QUARTER
+        for xx in self.piece_xs[piece]:
+
+            def body(i, xx=xx):
+                total = g[xx, self.c, pl.ds(pl.multiple_of(base + i, 16), 16), pl.ds(HALF, HALF)]
+                for k in range(1, NY):
+                    total += b["r1y"][k, xx, pl.ds(i, 16)].astype(jnp.float32)
+                b["a1y"][xx, pl.ds(i, 16)] = total
+                b["b2y"][xx, pl.ds(i, 16)] = total.astype(jnp.bfloat16)
+
+            chunks(QUARTER, 16, body)
+        for xx in self.piece_xs[piece]:
+
+            @pl.when(self.x != xx)
+            def _(xx=xx):
+                self.second_y(xx).start()
+
+    def from_x(self, recv, sems, like):
+        found = []
+        for k in (1, 3, 2):
+            source = lax.rem(self.x + k, NX)
+            found.append(send(like, recv.at[source], sems[0].at[source], sems[1].at[source], at(source, self.c, self.y, self.z)))
+        return found
+
+    def second_x_start(self):
+        b, g = self.b, self.g
+        for copy in self.from_x(b["r1x"], (b["s1x"], b["q1x"]), b["r1x"].at[0]):
+            copy.wait_recv()
+        for yy in range(NY):
+
+            def body(i, yy=yy):
+                total = g[self.x, self.c, pl.ds(yy * QUARTER + i, 16), pl.ds(0, HALF)]
+                for k in range(1, NX):
+                    source = lax.rem(self.x + k, NX)
+                    total += b["r1x"][source, pl.ds(yy * QUARTER + i, 16)].astype(jnp.float32)
+                b["a1x"][yy, pl.ds(i, 16)] = total
+                b["b2x"][yy, pl.ds(i, 16)] = total.astype(jnp.bfloat16)
+
+            chunks(QUARTER, 16, body)
+        for k in (2, 1, 3):
+            self.second_x(k).start()
+
+    def third(self, k):
+        b = self.b
+        to = lax.rem(self.z + k, NZ)
+        return send(
+            b["b3"].at[to],
+            b["r3"].at[k],
+            b["s3"].at[k],
+            b["q3"].at[k],
+            at(self.x, self.c, self.y, to),
+        )
+
+    def third_start(self):
+        b = self.b
+        for k in range(1, NY):
+            self.second_x(k).wait_recv()
+        for copy in self.from_x(b["r2y"], (b["s2y"], b["q2y"]), b["r2y"].at[0]):
+            copy.wait_recv()
+        for i in range(NZ):
+            rows = pl.ds(i * SHARE, SHARE)
+            left = b["a1x"][self.y, rows]
+            right = b["a1y"][self.x, rows]
+            for k in range(1, NY):
+                left += b["r2x"][k, rows].astype(jnp.float32)
+                right += b["r2y"][lax.rem(self.x + k, NX), rows].astype(jnp.float32)
+            both = jnp.concatenate([left, right], axis=1)
+            b["packed"][i, pl.ds(0, SHARE)] = both
+            b["b3"][i, pl.ds(0, SHARE)] = both.astype(jnp.bfloat16)
+        for k in (4, 3, 5, 2, 6, 1, 7):
+            self.third(k).start()
+
+    def finish(self, out):
+        b = self.b
+        for k in range(1, NZ):
+            self.third(k).wait_recv()
+        total = b["packed"][self.z, pl.ds(0, SHARE)]
+        for k in range(1, NZ):
+            total += b["r3"][k, pl.ds(0, SHARE)].astype(jnp.float32)
+        for j in range(WIDTH // 128):
+            out[pl.ds(j, SHARE, stride=WIDTH // 128), :] = total[:, 128 * j : 128 * j + 128]
+
+    def drain(self):
+        for piece in range(2):
+            for copy in self.core_copies(piece):
+                copy.wait_send()
+            for k in range(1, NY):
+                self.first_y(piece, k).wait_send()
+        for xx in range(NX):
+
+            @pl.when(self.x != xx)
+            def _(xx=xx):
+                self.first_x(xx).wait_send()
+                self.second_y(xx).wait_send()
+
+        for k in range(1, NY):
+            self.second_x(k).wait_send()
+        for k in range(1, NZ):
+            self.third(k).wait_send()
+
+    def vector_copies(self, stage):
+        b = self.b
+        x, c, y, z = self.x, self.c, self.y, self.z
+        if stage == 0:
+            return [send(b["vc"].at[0], b["vc"].at[1], b["us"].at[0], b["uq"].at[0], at(x, 1 - c, y, z))]
+        buf, base, count, me = (
+            (b["vx"], 1, NX, x),
+            (b["vy"], 1 + NX, NY, y),
+            (b["vz"], 1 + NX + NY, NZ, z),
+        )[stage - 1]
+        found = []
+        for k in range(1, count):
+            to = lax.rem(me + k, count)
+            device = (at(to, c, y, z), at(x, c, to, z), at(x, c, y, to))[stage - 1]
+            found.append((k, to, device, buf, base, me, count))
+        return [
+            send(buf.at[me], buf.at[me], b["us"].at[base + k], b["uq"].at[base + k], device)
+            for k, to, device, buf, base, me, count in found
+        ]
+
+    def vector_start(self, stage, value):
+        b = self.b
+        if stage == 0:
+            b["vc"][0] = value
+        else:
+            (b["vx"], b["vy"], b["vz"])[stage - 1][(self.x, self.y, self.z)[stage - 1]] = value
+        for copy in self.vector_copies(stage):
+            copy.start()
+
+    def vector_value(self, stage):
+        b = self.b
+        for copy in self.vector_copies(stage):
+            copy.wait_recv()
+        if stage == 0:
+            return b["vc"][0] + b["vc"][1]
+        buf = (b["vx"], b["vy"], b["vz"])[stage - 1]
+        total = buf[0]
+        for i in range(1, buf.shape[0]):
+            total += buf[i]
+        return total
+
+    def vector_drain(self):
+        for stage in range(4):
+            for copy in self.vector_copies(stage):
+                copy.wait_send()
+
+
+def reduce_all(inner_e, outer_e, inner_n, outer_n, vectors):
+    names = list(reduce_scratch())
+    sources = (inner_e, outer_e, inner_n, outer_n)
+
+    def kernel(e_in, e_out, n_in, n_out, vec, out, vec_out, g, load, *rest):
+        bufs = dict(zip(names, rest))
+        flat = g.reshape(NX * NC * BLOCK, WIDTH)
+        copies, row = [], 0
+        for i, ref in enumerate((e_in, e_out, n_in, n_out)):
+            rows = ref.shape[0]
+            copies.append(pltpu.make_async_copy(ref, flat.at[pl.ds(row, rows)], load.at[i]))
+            row += rows
+        for copy in copies:
+            copy.start()
+        entry_barrier()
+        red = Reducer(g, bufs)
+        red.vector_start(0, vec[...])
+        for copy in copies:
+            copy.wait()
+        for piece in range(2):
+            red.round_blocks(piece)
+            red.core_start(piece)
+        red.vector_start(1, red.vector_value(0))
+        for piece in range(2):
+            red.first_start(piece)
+        red.vector_start(2, red.vector_value(1))
+        for piece in range(2):
+            red.second_y_start(piece)
+        red.second_x_start()
+        red.vector_start(3, red.vector_value(2))
+        red.third_start()
+        vec_out[...] = red.vector_value(3)
+        red.finish(out)
+        red.drain()
+        red.vector_drain()
+
+    any_spec = pl.BlockSpec(memory_space=pl.ANY)
+    vmem_spec = pl.BlockSpec(memory_space=pltpu.VMEM)
+    return pl.pallas_call(
+        kernel,
+        out_shape=(
+            jax.ShapeDtypeStruct((SHARE * WIDTH // 128, 128), jnp.float32),
+            jax.ShapeDtypeStruct((8, WIDTH), jnp.float32),
+        ),
+        in_specs=[any_spec] * 4 + [vmem_spec],
+        out_specs=(vmem_spec, vmem_spec),
+        scratch_shapes=[
+            pltpu.VMEM((NX, NC, BLOCK, WIDTH), jnp.float32),
+            pltpu.SemaphoreType.DMA((4,)),
+            *reduce_scratch().values(),
+        ],
+        compiler_params=pltpu.CompilerParams(
+            collective_id=0, has_side_effects=True, vmem_limit_bytes=48 * 1024 * 1024
+        ),
+        name="reduce_weights",
+    )(*sources, vectors)
 
 
 def extended(block, sides, width):
@@ -139,15 +535,7 @@
         + contract_rows(pick_receiver, receiver_half)
         + from_rims
     )
-    flat_terms = jnp.concatenate(
-        [
-            (contract_rows(edge_inputs, epreact_half) * edge_norm).reshape(-1),
-            (contract_rows(edge_hidden, elinear_half) * edge_norm).reshape(-1),
-            (contract_rows(node_inputs, preact_half) * node_norm).reshape(-1),
-            (contract_rows(node_hidden, linear_half) * node_norm).reshape(-1),
-        ]
-    )
-    vector_terms = jnp.concatenate(
+    vector_terms = jnp.stack(
         [
             jnp.sum(epreact_back, axis=0) * edge_norm,
             jnp.sum(elinear_back, axis=0) * edge_norm,
@@ -157,10 +545,16 @@
             jnp.sum(cotan_node * node_normed, axis=0) * node_norm,
         ]
     )
-    grad_vectors = lax.psum(vector_terms, ("region", "patch"))
-    grad_weights = lax.psum_scatter(
-        flat_terms, ("region", "patch"), scatter_dimension=0, tiled=True
-    )
+    vectors = jnp.concatenate([vector_terms, jnp.zeros((2, feature_width), jnp.float32)], axis=0)
+    weights, vector_sums = reduce_all(
+        contract_rows(edge_inputs, epreact_half) * edge_norm,
+        contract_rows(edge_hidden, elinear_half) * edge_norm,
+        contract_rows(node_inputs, preact_half) * node_norm,
+        contract_rows(node_hidden, linear_half) * node_norm,
+        vectors,
+    )
+    grad_weights = weights.reshape(-1)
+    grad_vectors = vector_sums[:6].reshape(-1)
     return (grad_nodes, grad_edges, grad_weights, grad_vectors)
 
 

time: 340 us -> 99.2 us (0.29)
  the two profiles are of different devices: /device:TPU:2 before, /device:TPU:1 now
where the time goes in v1:
time: 99.2 us; the launch traced here: 98.6 us
  Pallas kernels  29.7 us (30%)
  matrix products  29.3 us (30%)
  local copies, waits for them, and re-layouts  19.1 us (19%)
  starting transfers between devices  13.8 us (14%)
  other arithmetic  5.75 us (6%)
    pallas_call x1, Pallas kernels, reduce_all(): pl.pallas_call(kernel, out_shape=(jax.ShapeDtypeStruct((SHARE * WIDTH //...  29.7 us
    unnamed x51, local copies, waits for them, and re-layouts  16 us
    dot_general x7, matrix products, contract_rows(): lax.dot_general(left, right, (((0,), (0,)), ((), ())), preferred_element_...  14.5 us
    ppermute x2, starting transfers between devices, extended(): lax.ppermute(lax.slice_in_dim(block, 0, width, axis=dim), axis, backward)  11.3 us
    convert_element_type x1, other arithmetic, per_device(): (fresh_back + einputs_back[:, :feature_width]).astype(jnp.bfloat16)  3.57 us
    dot_general x1, matrix products, per_device(): jnp.dot(epreact_half, edge_inner.T, preferred_element_type=jnp.float32)  3.51 us
    ppermute x2, starting transfers between devices, extended(): lax.ppermute(lax.slice_in_dim(block, block.shape[dim] - width, None, axis...  2.53 us
  transfers between devices with their start and end apart: 4, of which 0 were waited for; matrix products, arithmetic and copies ran while one was open for 10% of the time, Pallas kernels for 30%

profile of v1, /device:TPU:1, one launch (start us, length us, event | category | flops | bytes accessed | tf_op | source)
XLA Modules:
  0.0 98.6 jit_solution(2098153161177640111)
XLA Ops:
  1.5 1.2 %convolution_convert_fusion.2 = bf16[64,512]{1,0:T(8,128)(2,1)S(1)} fusion(bf16[256,512]{1,0:T(8,128)(2,1)} %param.17, s32[64]{0:T(128)S(1)} %eq.47), kind=kOutput, calls=%fused_computation.30 | convolution fusion | flops 16826368 | bytes 327936 | tf_op jit(solution)/shard_map/dot_general | solution.py:474
  2.7 2.5 %collective-permute-start = (bf16[1,32,512]{2,1,0:T(8,128)(2,1)S(1)}, bf16[1,32,512]{2,1,0:T(8,128)(2,1)S(1)}, u32[]{:S(2)}, u32[]{:S(2)}) collective-permute-start(bf16[1,32,512]{2,1,0:T(8,128)(2,1)S(1)} %get-tuple-element.26), channel_id=1, source_target_pairs={{0,1},{1,2},{2,3},{3,4},{4,5},{5,6},{6,7},{7,8},{8,9},{9,10},{10,1... | collective-permute-start | bytes 98312 | tf_op jit(solution)/shard_map/ppermute | solution.py:411
  5.2 6.5 %collective-permute-start.1 = (bf16[1,32,512]{2,1,0:T(8,128)(2,1)S(1)}, bf16[1,32,512]{2,1,0:T(8,128)(2,1)S(1)}, u32[]{:S(2)}, u32[]{:S(2)}) collective-permute-start(bf16[1,32,512]{2,1,0:T(8,128)(2,1)S(1)} %get-tuple-element.27), channel_id=1, source_target_pairs={{1,0},{2,1},{3,2},{4,3},{5,4},{6,5},{7,6},{8,7},{9,8},{10,9},{11,1... | collective-permute-start | bytes 98312 | tf_op jit(solution)/shard_map/ppermute | solution.py:414
  11.7 1.6 %convolution_convert_fusion = bf16[1024,512]{0,1:T(8,128)(2,1)S(1)} fusion(bf16[256,512]{1,0:T(8,128)(2,1)} %param.17, s32[1024]{0:T(1024)} %param.33), kind=kOutput, calls=%fused_computation.19 | convolution fusion | flops 269221888 | bytes 1314816 | tf_op jit(solution)/shard_map/dot_general | solution.py:483
  13.3 2.7 %copy.21 = bf16[1024,512]{0,1:T(8,128)(2,1)} copy(bf16[1024,512]{1,0:T(8,128)(2,1)} %param.18) | data formatting | bytes 2097152 | tf_op args[1]
  16.0 2.3 %copy.23 = bf16[1024,512]{0,1:T(8,128)(2,1)} copy(bf16[1024,512]{1,0:T(8,128)(2,1)} %param.20) | data formatting | bytes 2097152 | tf_op args[3]
  19.5 1.8 %fusion.3 = f32[1024,512]{1,0:T(8,128)S(1)} fusion(bf16[1536,512]{1,0:T(8,128)(2,1)S(1)} %copy-done, bf16[1024,512]{0,1:T(8,128)(2,1)S(1)} %convolution_convert_fusion, bf16[1024,512]{0,1:T(8,128)(2,1)S(1)} %fusion.2, bf16[1024,512]{0,1:T(8,128)(2,1)S(1)} %copy-done.11), kind=kOutput, calls=%fused_computation.23 | convolution fusion | flops 1620049920 | bytes 6815744 | tf_op jit(solution)/shard_map/dot_general | solution.py:487
  28.4 1.3 %multiply_reduce_fusion = (f32[512]{0:T(512)S(1)}, f32[1024]{0:T(1024)S(1)}, f32[1024]{0:T(1024)S(1)}, f32[1024,512]{0,1:T(8,128)S(1)}) fusion(f32[1024]{0:T(1024)S(1)} %add_rsqrt_fusion, f32[1024]{0:T(1024)S(1)} %broadcast_multiply_fusion.2, f32[1024,512]{0,1:T(8,128)S(1)} %get-tuple-element.29, f32[512]{0:T(512)S(1)} %copy-done.15, f32[512]{0:T(512)S(1)} %copy-done.16, ...), kind=kOutput, calls=%fused_computation.2 | convolution fusion | flops 274462208 | bytes 5531648 | tf_op jit(solution)/shard_map/dot_general | solution.py:507
  29.8 1.0 %fusion.54 = (f32[512]{0:T(512)S(1)}, bf16[1024,512]{0,1:T(8,128)(2,1)S(1)}) fusion(f32[1024]{0:T(1024)S(1)} %broadcast_multiply_fusion, f32[1024]{0:T(1024)S(1)} %broadcast_multiply_fusion.2, f32[1024,512]{0,1:T(8,128)S(1)} %get-tuple-element.29, f32[512]{0:T(512)S(1)} %copy-done.15, f32[1024]{0:T(1024)S(1)} %broadcast_multiply_fusion.1, ...), kind=kLoop, calls=%fused_computation.111 | loop fusion | flops 5242368 | bytes 5265408 | tf_op jit(solution)/shard_map/reduce_sum | solution.py:541
  31.1 1.8 %convolution_multiply_fusion.2.e_out = f32[512,512]{1,0:T(8,128)} fusion(bf16[1024,512]{0,1:T(8,128)(2,1)S(1)} %get-tuple-element.21, f32[1024,512]{1,0:T(8,128)S(1)} %fusion.3, f32[512]{0:T(512)S(1)} %copy-done.22), kind=kOutput, calls=%fused_computation.21 | convolution fusion | flops 540278784 | bytes 4196352 | tf_op jit(solution)/shard_map/dot_general | solution.py:440
  32.9 1.3 %fusion.58 = (f32[512]{0:T(512)S(1)}, bf16[1024,512]{1,0:T(8,128)(2,1)S(1)}) fusion(f32[1024,512]{1,0:T(8,128)S(1)} %fusion.3, f32[512]{0:T(512)S(1)} %copy-done.22, bf16[512,512]{1,0:T(8,128)(2,1)S(1)} %copy-done.18, bf16[1024,512]{0,1:T(8,128)(2,1)S(1)} %get-tuple-element.21), kind=kOutput, calls=%fused_computation.115 | convolution fusion | flops 542637568 | bytes 4722688 | tf_op jit(solution)/shard_map/dot_general | solution.py:512
  34.3 1.8 %convolution_multiply_fusion.1.n_in = f32[1024,512]{1,0:T(8,128)} fusion(bf16[256,512]{1,0:T(8,128)(2,1)S(1)} %convolution_convert_fusion.1, bf16[256,512]{1,0:T(8,128)(2,1)S(1)} %copy-done.6, bf16[256,512]{1,0:T(8,128)(2,1)S(1)} %get-tuple-element.40), kind=kOutput, calls=%fused_computation.15 | convolution fusion | flops 270008320 | bytes 2883584 | tf_op jit(solution)/shard_map/dot_general | solution.py:440
  36.1 3.8 %convolution_multiply_fusion.e_in = f32[1536,512]{1,0:T(8,128)} fusion(bf16[1024,512]{0,1:T(8,128)(2,1)S(1)} %copy-done.9, bf16[1024,512]{0,1:T(8,128)(2,1)S(1)} %fusion.2, bf16[1024,512]{0,1:T(8,128)(2,1)S(1)} %copy-done.11, bf16[1024,512]{1,0:T(8,128)(2,1)S(1)} %get-tuple-element.38), kind=kOutput, calls=%fused_computation | convolution fusion | flops 1620836352 | bytes 7340032 | tf_op jit(solution)/shard_map/dot_general | solution.py:440
  39.9 3.5 %fusion.56 = (bf16[1024,1536]{1,0:T(8,128)(2,1)}, f32[1024,1536]{1,0:T(8,128)S(1)}) fusion(bf16[1536,512]{1,0:T(8,128)(2,1)S(1)} %copy-done, bf16[1024,512]{1,0:T(8,128)(2,1)S(1)} %get-tuple-element.38), kind=kOutput, calls=%fused_computation.113 | convolution fusion | flops 1612185600 | bytes 12058624 | tf_op jit(solution)/shard_map/dot_general | solution.py:516
  43.4 1.5 %slice.88 = f32[1024,512]{1,0:T(8,128)} slice(f32[1024,1536]{1,0:T(8,128)S(1)} %get-tuple-element.34), slice={[0:1024], [0:512]} | slice | bytes 4194304 | tf_op jit(solution)/shard_map/slice | solution.py:517
  44.9 2.9 %copy.28 = f32[1024,512]{0,1:T(8,128)} copy(f32[1024,512]{1,0:T(8,128)} %slice.88) | data formatting | bytes 4194304
  47.8 3.6 %add_convert_fusion = bf16[1024,512]{0,1:T(8,128)(2,1)} fusion(f32[1024,512]{0,1:T(8,128)} %copy-done.3, f32[1024,512]{0,1:T(8,128)} %copy.28), kind=kLoop, calls=%fused_computation.3 | loop fusion | flops 1048576 | bytes 5242880 | tf_op jit(solution)/shard_map/convert_element_type | solution.py:517
  51.4 3.0 %fusion.57 = (bf16[320,512]{1,0:T(8,128)(2,1)S(1)}, f32[320,512]{1,0:T(8,128)}) fusion(bf16[1024,1536]{1,0:T(8,128)(2,1)} %get-tuple-element.33, s32[1024]{0:T(1024)S(1)} %copy-done.19), kind=kOutput, calls=%fused_computation.114 | convolution fusion | flops 336035840 | bytes 2035712 | tf_op jit(solution)/shard_map/dot_general | solution.py:440
  54.3 4.8 %collective-permute-start.3 = (bf16[1,32,512]{2,1,0:T(8,128)(2,1)S(1)}, bf16[1,32,512]{2,1,0:T(8,128)(2,1)S(1)}, u32[]{:S(2)}, u32[]{:S(2)}) collective-permute-start(bf16[1,32,512]{2,1,0:T(8,128)(2,1)S(1)} %get-tuple-element.23), channel_id=1, source_target_pairs={{1,0},{2,1},{3,2},{4,3},{5,4},{6,5},{7,6},{8,7},{9,8},{10,9},{11,1... | collective-permute-start | bytes 98312 | tf_op jit(solution)/shard_map/ppermute | solution.py:414
  59.2 1.6 %copy-done.1 = f32[1024,512]{1,0:T(8,128)S(1)} copy-done((f32[1024,512]{1,0:T(8,128)S(1)}, f32[1024,512]{1,0:T(8,128)}, u32[]{:S(2)}) %copy-start.1) | copy-done | bytes 2097176
  60.8 1.2 %copy-done.2 = f32[512,512]{1,0:T(8,128)S(1)} copy-done((f32[512,512]{1,0:T(8,128)S(1)}, f32[512,512]{1,0:T(8,128)}, u32[]{:S(2)}) %copy-start.2) | copy-done | bytes 1048600
  62.0 29.7 %reduce_weights.1 = (f32[56,128]{1,0:T(8,128)S(1)}, f32[8,512]{1,0:T(8,128)S(1)}) custom-call(f32[1536,512]{1,0:T(8,128)} %convolution_multiply_fusion.e_in, f32[512,512]{1,0:T(8,128)S(1)} %copy-done.2, f32[1024,512]{1,0:T(8,128)S(1)} %copy-done.1, f32[512,512]{1,0:T(8,128)S(1)} %convolution_multiply_fusion.3.n_out, f32[8,512]{1,0:T(8,128)S(1)} %concatenate.23.vec), custom_call_target="tpu_custom_call" | custom-call | tf_op jit(solution)/shard_map/reduce_weights/pallas_call | solution.py:385
  92.3 2.3 %copy.26 = bf16[1024,512]{1,0:T(8,128)(2,1)} copy(bf16[1024,512]{0,1:T(8,128)(2,1)} %add_convert_fusion) | data formatting | bytes 2097152
  95.1 2.9 %fusion.4 = f32[256,512]{1,0:T(8,128)} fusion(f32[256,512]{1,0:T(8,128)S(1)} %fusion.34, bf16[1024,1536]{1,0:T(8,128)(2,1)} %get-tuple-element.33, bf16[256,512]{1,0:T(8,128)(2,1)S(1)} %copy-done.7, f32[320,512]{1,0:T(8,128)} %get-tuple-element.36, f32[256,1024]{1,0:T(8,128)S(1)} %copy-done.5, s32[1024]{0:T(1024)S(1)} %copy-done.13), kind=kOutput, calls=%fused_computation.26 | convolution fusion | flops 269352960 | bytes 3411968 | tf_op jit(solution)/shard_map/dot_general | solution.py:440
  (84 shorter events, 11.2 us)
Async XLA Ops:
  0.6 18.5 %copy-start = (bf16[1536,512]{1,0:T(8,128)(2,1)S(1)}, bf16[1536,512]{1,0:T(8,128)(2,1)}, u32[]{:S(2)}) copy-start(bf16[1536,512]{1,0:T(8,128)(2,1)} %param.21) | copy-start | bytes 4718596
  2.7 15.6 %collective-permute-start = (bf16[1,32,512]{2,1,0:T(8,128)(2,1)S(1)}, bf16[1,32,512]{2,1,0:T(8,128)(2,1)S(1)}, u32[]{:S(2)}, u32[]{:S(2)}) collective-permute-start(bf16[1,32,512]{2,1,0:T(8,128)(2,1)S(1)} %get-tuple-element.26), channel_id=1, source_target_pairs={{0,1},{1,2},{2,3},{3,4},{4,5},{5,6},{6,7},{7,8},{8,9},{9,10},{10,1... | collective-permute-start | bytes 98312 | tf_op jit(solution)/shard_map/ppermute | solution.py:411
  5.2 13.0 %collective-permute-start.1 = (bf16[1,32,512]{2,1,0:T(8,128)(2,1)S(1)}, bf16[1,32,512]{2,1,0:T(8,128)(2,1)S(1)}, u32[]{:S(2)}, u32[]{:S(2)}) collective-permute-start(bf16[1,32,512]{2,1,0:T(8,128)(2,1)S(1)} %get-tuple-element.27), channel_id=1, source_target_pairs={{1,0},{2,1},{3,2},{4,3},{5,4},{6,5},{7,6},{8,7},{9,8},{10,9},{11,1... | collective-permute-start | bytes 98312 | tf_op jit(solution)/shard_map/ppermute | solution.py:414
  13.3 5.9 %copy-start.8 = (bf16[1024,512]{0,1:T(8,128)(2,1)}, bf16[1024,512]{0,1:T(8,128)(2,1)S(1)}, u32[]{:S(2)}) copy-start(bf16[1024,512]{0,1:T(8,128)(2,1)S(1)} %convolution_convert_fusion) | copy-start | bytes 3145732
  13.3 5.0 %copy-start.6 = (bf16[256,512]{1,0:T(8,128)(2,1)S(1)}, bf16[256,512]{1,0:T(8,128)(2,1)}, u32[]{:S(2)}) copy-start(bf16[256,512]{1,0:T(8,128)(2,1)} %param.17) | copy-start | bytes 786436
  13.3 5.0 %copy-start.19 = (s32[1024]{0:T(1024)S(1)}, s32[1024]{0:T(1024)}, u32[]{:S(2)}) copy-start(s32[1024]{0:T(1024)} %param.32) | copy-start | bytes 12292
  18.2 1.2 %copy-start.11 = (bf16[1024,512]{0,1:T(8,128)(2,1)S(1)}, bf16[1024,512]{0,1:T(8,128)(2,1)}, u32[]{:S(2)}) copy-start(bf16[1024,512]{0,1:T(8,128)(2,1)} %copy.21) | copy-start | bytes 3145732
  19.5 1.8 %copy-start.15 = (f32[512]{0:T(512)S(1)}, f32[512]{0:T(512)}, u32[]{:S(2)}) copy-start(f32[512]{0:T(512)} %param.26) | copy-start | bytes 6148
  19.5 1.9 %copy-start.18 = (bf16[512,512]{1,0:T(8,128)(2,1)S(1)}, bf16[512,512]{1,0:T(8,128)(2,1)}, u32[]{:S(2)}) copy-start(bf16[512,512]{1,0:T(8,128)(2,1)} %param.22) | copy-start | bytes 1572868
  19.5 1.9 %copy-start.22 = (f32[512]{0:T(512)S(1)}, f32[512]{0:T(512)}, u32[]{:S(2)}) copy-start(f32[512]{0:T(512)} %param.25) | copy-start | bytes 6148
  23.0 1.2 %copy-start.10 = (bf16[1024,512]{1,0:T(8,128)(2,1)S(1)}, bf16[1024,512]{1,0:T(8,128)(2,1)}, u32[]{:S(2)}) copy-start(bf16[1024,512]{1,0:T(8,128)(2,1)} %param.23) | copy-start | bytes 3145732
  23.0 1.2 %copy-start.20 = (f32[512]{0:T(512)S(1)}, f32[512]{0:T(512)}, u32[]{:S(2)}) copy-start(f32[512]{0:T(512)} %param.28) | copy-start | bytes 6148
  24.2 1.0 %copy-start.17 = (bf16[512,512]{1,0:T(8,128)(2,1)S(1)}, bf16[512,512]{1,0:T(8,128)(2,1)}, u32[]{:S(2)}) copy-start(bf16[512,512]{1,0:T(8,128)(2,1)} %param.24) | copy-start | bytes 1572868
  24.2 1.0 %copy-start.21 = (f32[512]{0:T(512)S(1)}, f32[512]{0:T(512)}, u32[]{:S(2)}) copy-start(f32[512]{0:T(512)} %param.29) | copy-start | bytes 6148
  25.3 1.0 copy-start.14
  27.2 1.2 %copy-start.12 = (bf16[1024,512]{0,1:T(8,128)(2,1)S(1)}, bf16[1024,512]{0,1:T(8,128)(2,1)}, u32[]{:S(2)}) copy-start(bf16[1024,512]{0,1:T(8,128)(2,1)} %copy.23) | copy-start | bytes 3145732
  28.4 1.3 %copy-start.4 = (f32[256,1024]{1,0:T(8,128)}, f32[256,1024]{1,0:T(8,128)S(1)}, u32[]{:S(2)}) copy-start(f32[256,1024]{1,0:T(8,128)S(1)} %fusion.39) | copy-start | bytes 3145732
  29.8 1.4 %copy-start.3 = (f32[1024,512]{0,1:T(8,128)}, f32[1024,512]{0,1:T(8,128)S(1)}, u32[]{:S(2)}) copy-start(f32[1024,512]{0,1:T(8,128)S(1)} %get-tuple-element.32) | copy-start | bytes 6291460
  34.2 1.8 %copy-start.9 = (bf16[1024,512]{0,1:T(8,128)(2,1)S(1)}, bf16[1024,512]{0,1:T(8,128)(2,1)}, u32[]{:S(2)}) copy-start(bf16[1024,512]{0,1:T(8,128)(2,1)} %copy-done.8) | copy-start | bytes 3145732
  54.3 40.2 %collective-permute-start.2 = (bf16[1,32,512]{2,1,0:T(8,128)(2,1)S(1)}, bf16[1,32,512]{2,1,0:T(8,128)(2,1)S(1)}, u32[]{:S(2)}, u32[]{:S(2)}) collective-permute-start(bf16[1,32,512]{2,1,0:T(8,128)(2,1)S(1)} %get-tuple-element.22), channel_id=1, source_target_pairs={{0,1},{1,2},{2,3},{3,4},{4,5},{5,6},{6,7},{7,8},{8,9},{9,10},{10,1... | collective-permute-start | bytes 98312 | tf_op jit(solution)/shard_map/ppermute | solution.py:411
  54.3 40.2 %collective-permute-start.3 = (bf16[1,32,512]{2,1,0:T(8,128)(2,1)S(1)}, bf16[1,32,512]{2,1,0:T(8,128)(2,1)S(1)}, u32[]{:S(2)}, u32[]{:S(2)}) collective-permute-start(bf16[1,32,512]{2,1,0:T(8,128)(2,1)S(1)} %get-tuple-element.23), channel_id=1, source_target_pairs={{1,0},{2,1},{3,2},{4,3},{5,4},{6,5},{7,6},{8,7},{9,8},{10,9},{11,1... | collective-permute-start | bytes 98312 | tf_op jit(solution)/shard_map/ppermute | solution.py:414
  59.2 1.6 %copy-start.1 = (f32[1024,512]{1,0:T(8,128)S(1)}, f32[1024,512]{1,0:T(8,128)}, u32[]{:S(2)}) copy-start(f32[1024,512]{1,0:T(8,128)} %convolution_multiply_fusion.1.n_in) | copy-start | bytes 6291460
  60.8 1.2 %copy-start.2 = (f32[512,512]{1,0:T(8,128)S(1)}, f32[512,512]{1,0:T(8,128)}, u32[]{:S(2)}) copy-start(f32[512,512]{1,0:T(8,128)} %convolution_multiply_fusion.2.e_out) | copy-start | bytes 3145732
  91.7 3.4 %copy-start.5 = (f32[256,1024]{1,0:T(8,128)S(1)}, f32[256,1024]{1,0:T(8,128)}, u32[]{:S(2)}) copy-start(f32[256,1024]{1,0:T(8,128)} %copy-done.4) | copy-start | bytes 3145732
  (3 other events, 2.3 us)

commit v2 on v1

v2 whole, which is shorter than its diff:
```python
import math
from types import SimpleNamespace

import jax
import jax.numpy as jnp
from jax import lax
from jax.experimental import pallas as pl
from jax.experimental.pallas import tpu as pltpu
from jax.sharding import PartitionSpec as P

MESH = pl.DeviceIdType.MESH
NX, NC, NY, NZ = 4, 2, 4, 8
WIDTH, HALF = 512, 256
BLOCK, QUARTER, SHARE, PAD = 448, 112, 14, 16


def coordinates():
    region, patch = lax.axis_index("region"), lax.axis_index("patch")
    return region // NC, lax.rem(region, NC), patch // NZ, lax.rem(patch, NZ)


def at(x, c, y, z):
    return (x * NC + c, y * NZ + z)


def beside(step):
    region, patch = lax.axis_index("region"), lax.axis_index("patch")
    return (region, lax.rem(patch + step + NY * NZ, NY * NZ))


def peers():
    x, c, y, z = coordinates()
    found = [at(x, 1 - c, y, z), beside(1), beside(-1)]
    found += [at(lax.rem(x + k, NX), c, y, z) for k in range(1, NX)]
    found += [at(x, c, lax.rem(y + k, NY), z) for k in range(1, NY)]
    found += [at(x, c, y, lax.rem(z + k, NZ)) for k in range(1, NZ)]
    return found


def barrier_signal():
    barrier = pltpu.get_barrier_semaphore()
    for device in peers():
        pl.semaphore_signal(barrier, inc=1, device_id=device, device_id_type=MESH)


def barrier_wait():
    pl.semaphore_wait(pltpu.get_barrier_semaphore(), len(peers()))


def send(src, dst, send_sem, recv_sem, device):
    return pltpu.make_async_remote_copy(
        src_ref=src,
        dst_ref=dst,
        send_sem=send_sem,
        recv_sem=recv_sem,
        device_id=device,
        device_id_type=MESH,
    )


def chunks(total, step, body):
    def one(i, carry):
        body(pl.multiple_of(i * step, step))
        return carry

    lax.fori_loop(0, total // step, one, 0)


def reduce_scratch():
    bf16, f32 = jnp.bfloat16, jnp.float32
    dma = pltpu.SemaphoreType.DMA
    return dict(
        sb=pltpu.VMEM((NX, NC, BLOCK, WIDTH), bf16),
        r0=pltpu.VMEM((NX, BLOCK, WIDTH), bf16),
        b1=pltpu.VMEM((NX, BLOCK, WIDTH), bf16),
        r1x=pltpu.VMEM((NX, BLOCK, HALF), bf16),
        r1y=pltpu.VMEM((NY, NX, QUARTER, HALF), bf16),
        a1x=pltpu.VMEM((NY, QUARTER, HALF), f32),
        b2x=pltpu.VMEM((NY, QUARTER, HALF), bf16),
        r2x=pltpu.VMEM((NY, QUARTER, HALF), bf16),
        a1y=pltpu.VMEM((NX, QUARTER, HALF), f32),
        b2y=pltpu.VMEM((NX, QUARTER, HALF), bf16),
        r2y=pltpu.VMEM((NX, QUARTER, HALF), bf16),
        packed=pltpu.VMEM((NZ, PAD, WIDTH), f32),
        b3=pltpu.VMEM((NZ, PAD, WIDTH), bf16),
        r3=pltpu.VMEM((NZ, PAD, WIDTH), bf16),
        s0=dma((NX,)),
        q0=dma((NX,)),
        s1x=dma((NX,)),
        q1x=dma((NX,)),
        s1y=dma((3, NY)),
        q1y=dma((3, NY)),
        s2x=dma((NY,)),
        q2x=dma((NY,)),
        s2y=dma((NX,)),
        q2y=dma((NX,)),
        s3=dma((NZ,)),
        q3=dma((NZ,)),
        vc=pltpu.VMEM((2, 8, WIDTH), f32),
        vx=pltpu.VMEM((NX, 8, WIDTH), f32),
        vy=pltpu.VMEM((NY, 8, WIDTH), f32),
        vz=pltpu.VMEM((NZ, 8, WIDTH), f32),
        us=dma((1 + NX + NY + NZ,)),
        uq=dma((1 + NX + NY + NZ,)),
    )


class Reducer:
    def __init__(self, g, bufs):
        self.g, self.b = g, bufs
        self.x, self.c, self.y, self.z = coordinates()
        self.piece_xs = ((3,), (2,), (0, 1))

    def core_copies(self, piece):
        b = self.b
        return [
            send(
                b.sb.at[xx, 1 - self.c],
                b.r0.at[xx],
                b.s0.at[xx],
                b.q0.at[xx],
                at(self.x, 1 - self.c, self.y, self.z),
            )
            for xx in self.piece_xs[piece]
        ]

    def core_start(self, piece):
        for copy in self.core_copies(piece):
            copy.start()

    def round_blocks(self, piece):
        b, g = self.b, self.g
        for xx in self.piece_xs[piece]:
            for cc in range(NC):

                def body(i, xx=xx, cc=cc):
                    b.sb[xx, cc, pl.ds(i, 64)] = g[xx, cc, pl.ds(i, 64)].astype(jnp.bfloat16)

                chunks(BLOCK, 64, body)

    def first_x(self, xx):
        b = self.b
        return send(
            b.b1.at[xx, :, pl.ds(0, HALF)],
            b.r1x.at[self.x],
            b.s1x.at[xx],
            b.q1x.at[self.x],
            at(xx, self.c, self.y, self.z),
        )

    def first_y(self, piece, k):
        b = self.b
        to = lax.rem(self.y + k, NY)
        xs = self.piece_xs[piece]
        blocks = pl.ds(xs[0], len(xs))
        return send(
            b.b1.at[blocks, pl.ds(pl.multiple_of(to * QUARTER, 16), QUARTER), pl.ds(HALF, HALF)],
            b.r1y.at[k, blocks],
            b.s1y.at[piece, k],
            b.q1y.at[piece, k],
            at(self.x, self.c, to, self.z),
        )

    def first_start(self, piece):
        b, g = self.b, self.g
        for copy in self.core_copies(piece):
            copy.wait_recv()
        for xx in self.piece_xs[piece]:

            def body(i, xx=xx):
                total = g[xx, self.c, pl.ds(i, 64)] + b.r0[xx, pl.ds(i, 64)].astype(jnp.float32)
                g[xx, self.c, pl.ds(i, 64)] = total
                b.b1[xx, pl.ds(i, 64)] = total.astype(jnp.bfloat16)

            chunks(BLOCK, 64, body)
        for k in (2, 1, 3):
            self.first_y(piece, k).start()
        for xx in self.piece_xs[piece]:

            @pl.when(self.x != xx)
            def _(xx=xx):
                self.first_x(xx).start()

    def second_x(self, k):
        b = self.b
        to = lax.rem(self.y + k, NY)
        return send(
            b.b2x.at[to],
            b.r2x.at[k],
            b.s2x.at[k],
            b.q2x.at[k],
            at(self.x, self.c, to, self.z),
        )

    def second_y(self, xx):
        b = self.b
        return send(
            b.b2y.at[xx],
            b.r2y.at[self.x],
            b.s2y.at[xx],
            b.q2y.at[self.x],
            at(xx, self.c, self.y, self.z),
        )

    def second_y_start(self, piece):
        b, g = self.b, self.g
        for k in (1, 3, 2):
            self.first_y(piece, k).wait_recv()
        base = self.y * QUARTER
        for xx in self.piece_xs[piece]:

            def body(i, xx=xx):
                total = g[xx, self.c, pl.ds(pl.multiple_of(base + i, 16), 16), pl.ds(HALF, HALF)]
                for k in range(1, NY):
                    total += b.r1y[k, xx, pl.ds(i, 16)].astype(jnp.float32)
                b.a1y[xx, pl.ds(i, 16)] = total
                b.b2y[xx, pl.ds(i, 16)] = total.astype(jnp.bfloat16)

            chunks(QUARTER, 16, body)
        for xx in self.piece_xs[piece]:

            @pl.when(self.x != xx)
            def _(xx=xx):
                self.second_y(xx).start()

    def from_x(self, recv, sems, like):
        found = []
        for k in (1, 3, 2):
            source = lax.rem(self.x + k, NX)
            found.append(send(like, recv.at[source], sems[0].at[source], sems[1].at[source], at(source, self.c, self.y, self.z)))
        return found

    def second_x_start(self):
        b, g = self.b, self.g
        for copy in self.from_x(b.r1x, (b.s1x, b.q1x), b.r1x.at[0]):
            copy.wait_recv()
        for yy in range(NY):

            def body(i, yy=yy):
                total = g[self.x, self.c, pl.ds(yy * QUARTER + i, 16), pl.ds(0, HALF)]
                for k in range(1, NX):
                    source = lax.rem(self.x + k, NX)
                    total += b.r1x[source, pl.ds(yy * QUARTER + i, 16)].astype(jnp.float32)
                b.a1x[yy, pl.ds(i, 16)] = total
                b.b2x[yy, pl.ds(i, 16)] = total.astype(jnp.bfloat16)

            chunks(QUARTER, 16, body)
        for k in (2, 1, 3):
            self.second_x(k).start()

    def third(self, k):
        b = self.b
        to = lax.rem(self.z + k, NZ)
        return send(
            b.b3.at[to],
            b.r3.at[k],
            b.s3.at[k],
            b.q3.at[k],
            at(self.x, self.c, self.y, to),
        )

    def third_start(self):
        b = self.b
        for k in range(1, NY):
            self.second_x(k).wait_recv()
        for copy in self.from_x(b.r2y, (b.s2y, b.q2y), b.r2y.at[0]):
            copy.wait_recv()
        for i in range(NZ):
            rows = pl.ds(i * SHARE, SHARE)
            left = b.a1x[self.y, rows]
            right = b.a1y[self.x, rows]
            for k in range(1, NY):
                left += b.r2x[k, rows].astype(jnp.float32)
                right += b.r2y[lax.rem(self.x + k, NX), rows].astype(jnp.float32)
            both = jnp.concatenate([left, right], axis=1)
            b.packed[i, pl.ds(0, SHARE)] = both
            b.b3[i, pl.ds(0, SHARE)] = both.astype(jnp.bfloat16)
        for k in (4, 3, 5, 2, 6, 1, 7):
            self.third(k).start()

    def finish(self, out):
        b = self.b
        for k in range(1, NZ):
            self.third(k).wait_recv()
        total = b.packed[self.z, pl.ds(0, SHARE)]
        for k in range(1, NZ):
            total += b.r3[k, pl.ds(0, SHARE)].astype(jnp.float32)
        for j in range(WIDTH // 128):
            out[pl.ds(j, SHARE, stride=WIDTH // 128), :] = total[:, 128 * j : 128 * j + 128]

    def drain(self):
        for piece in range(len(self.piece_xs)):
            for copy in self.core_copies(piece):
                copy.wait_send()
            for k in range(1, NY):
                self.first_y(piece, k).wait_send()
        for xx in range(NX):

            @pl.when(self.x != xx)
            def _(xx=xx):
                self.first_x(xx).wait_send()
                self.second_y(xx).wait_send()

        for k in range(1, NY):
            self.second_x(k).wait_send()
        for k in range(1, NZ):
            self.third(k).wait_send()

    def vector_copies(self, stage):
        b = self.b
        x, c, y, z = self.x, self.c, self.y, self.z
        if stage == 0:
            return [send(b.vc.at[0], b.vc.at[1], b.us.at[0], b.uq.at[0], at(x, 1 - c, y, z))]
        buf, base, count, me = (
            (b.vx, 1, NX, x),
            (b.vy, 1 + NX, NY, y),
            (b.vz, 1 + NX + NY, NZ, z),
        )[stage - 1]
        found = []
        for k in range(1, count):
            to = lax.rem(me + k, count)
            device = (at(to, c, y, z), at(x, c, to, z), at(x, c, y, to))[stage - 1]
            found.append((k, to, device, buf, base, me, count))
        return [
            send(buf.at[me], buf.at[me], b.us.at[base + k], b.uq.at[base + k], device)
            for k, to, device, buf, base, me, count in found
        ]

    def vector_start(self, stage, value=None):
        b = self.b
        if stage > 0:
            (b.vx, b.vy, b.vz)[stage - 1][(self.x, self.y, self.z)[stage - 1]] = value
        for copy in self.vector_copies(stage):
            copy.start()

    def vector_value(self, stage):
        b = self.b
        for copy in self.vector_copies(stage):
            copy.wait_recv()
        if stage == 0:
            return b.vc[0] + b.vc[1]
        buf = (b.vx, b.vy, b.vz)[stage - 1]
        total = buf[0]
        for i in range(1, buf.shape[0]):
            total += buf[i]
        return total

    def vector_drain(self):
        for stage in range(4):
            for copy in self.vector_copies(stage):
                copy.wait_send()


NODES, EDGES, SLOTS, LOOKUP, PICKS = 256, 1024, 32, 320, 640
TILE = 512


def dot(left, right):
    return jnp.dot(left, right, preferred_element_type=jnp.float32)


def dot_nt(left, right):
    return lax.dot_general(left, right, (((1,), (1,)), ((), ())), preferred_element_type=jnp.float32)


def dot_tn(left, right):
    return lax.dot_general(left, right, (((0,), (0,)), ((), ())), preferred_element_type=jnp.float32)


def layer_norm(values):
    centred = values - jnp.mean(values, axis=-1, keepdims=True)
    invstd = lax.rsqrt(jnp.mean(centred * centred, axis=-1, keepdims=True) + 1e-05)
    return centred * invstd, invstd


def norm_back(upstream, normed, invstd, gains):
    scaled = upstream * gains
    return invstd * (
        scaled
        - jnp.mean(scaled, axis=-1, keepdims=True)
        - normed * jnp.mean(scaled * normed, axis=-1, keepdims=True)
    )


def silu_parts(preact):
    sigmoid = 1.0 / (1.0 + jnp.exp(-preact))
    return preact * sigmoid, sigmoid * (1.0 + preact * (1.0 - sigmoid))


def column_sums(values):
    return jnp.sum(values.reshape(-1, 8, WIDTH), axis=0)


def operands_named(
    nodes, edges, ncot, ecot, wei, weo, wni, wno, eshift, eoff, egain, nshift, noff, ngain, sendid, sndid, rcvid
):
    return SimpleNamespace(**locals())


SMALL = ("eshift", "eoff", "egain", "nshift", "noff", "ngain", "sendid", "sndid", "rcvid")


def compute_scratch():
    bf16, f32 = jnp.bfloat16, jnp.float32
    vm, dma = pltpu.VMEM, pltpu.SemaphoreType.DMA
    return dict(
        g=vm((NX, NC, BLOCK, WIDTH), f32),
        look=vm((LOOKUP, WIDTH), bf16),
        edges_v=vm((EDGES, WIDTH), bf16),
        ncot_v=vm((NODES, WIDTH), bf16),
        ecot_v=vm((EDGES, WIDTH), bf16),
        wei_v=vm((3 * WIDTH, WIDTH), bf16),
        weo_v=vm((WIDTH, WIDTH), bf16),
        wni_v=vm((2 * WIDTH, WIDTH), bf16),
        wno_v=vm((WIDTH, WIDTH), bf16),
        eshift_v=vm((1, WIDTH), f32),
        eoff_v=vm((1, WIDTH), f32),
        egain_v=vm((1, WIDTH), f32),
        nshift_v=vm((1, WIDTH), f32),
        noff_v=vm((1, WIDTH), f32),
        ngain_v=vm((1, WIDTH), f32),
        sendid_v=vm((2, SLOTS), jnp.int32),
        sndid_v=vm((EDGES // 128, 128), jnp.int32),
        rcvid_v=vm((EDGES // 128, 128), jnp.int32),
        loads=dma((18,)),
        pick=vm((EDGES, PICKS), bf16),
        pick_t=vm((PICKS, EDGES), bf16),
        proj=vm((PICKS, WIDTH), bf16),
        outgoing=vm((2 * SLOTS, WIDTH), bf16),
        pre=vm((EDGES, WIDTH), f32),
        dact=vm((EDGES, WIDTH), f32),
        hidden=vm((EDGES, WIDTH), bf16),
        normed=vm((EDGES, WIDTH), f32),
        invstd=vm((EDGES, 128), f32),
        agg=vm((NODES, WIDTH), f32),
        agg_b=vm((NODES, WIDTH), bf16),
        back_b=vm((NODES, WIDTH), bf16),
        nhid=vm((NODES, WIDTH), bf16),
        lhalf=vm((NODES, WIDTH), bf16),
        phalf=vm((NODES, WIDTH), bf16),
        elhalf=vm((EDGES, WIDTH), bf16),
        ephalf=vm((EDGES, WIDTH), bf16),
        gathered=vm((PICKS, WIDTH), bf16),
        rim=vm((2 * SLOTS, WIDTH), bf16),
        back=vm((2 * SLOTS, WIDTH), bf16),
        gnodes=vm((NODES, WIDTH), f32),
        sums=vm((3, 8, WIDTH), f32),
        hs=dma((4,)),
        hq=dma((4,)),
    )


def layer(edge_norm, node_norm, *operands):
    names = list(compute_scratch())
    comm_names = list(reduce_scratch())

    def kernel(*refs):
        given = operands_named(*refs[:17])
        gn_out, ge_out, w_out, v_out = refs[17:21]
        s = SimpleNamespace(**dict(zip(names, refs[21 : 21 + len(names)])))
        bufs = SimpleNamespace(**dict(zip(comm_names, refs[21 + len(names) :])))
        bf16, f32 = jnp.bfloat16, jnp.float32
        barrier_signal()
        red = Reducer(s.g, bufs)
        flat = s.g.reshape(NX * NC * BLOCK, WIDTH)
        wei = given.wei
        loads = dict(
            ecot=(given.ecot, s.ecot_v),
            ncot=(given.ncot, s.ncot_v),
            wno=(given.wno, s.wno_v),
            wni=(given.wni, s.wni_v),
            weo=(given.weo, s.weo_v),
            ws=(wei.at[pl.ds(WIDTH, 2 * WIDTH)], s.wei_v.at[pl.ds(WIDTH, 2 * WIDTH)]),
            edges=(given.edges, s.edges_v),
            we=(wei.at[pl.ds(0, WIDTH)], s.wei_v.at[pl.ds(0, WIDTH)]),
            nodes=(given.nodes, s.look.at[pl.ds(0, NODES)]),
        )
        for name in SMALL:
            loads[name] = (getattr(given, name), getattr(s, name + "_v"))
            setattr(given, name, getattr(s, name + "_v"))
        load = {}
        for i, (name, (src, dst)) in enumerate(reversed(loads.items())):
            load[name] = pltpu.make_async_copy(src, dst, s.loads.at[i])
            load[name].start()
        load = SimpleNamespace(**load)
        w_e = s.wei_v.at[pl.ds(0, WIDTH)]
        w_s = s.wei_v.at[pl.ds(WIDTH, WIDTH)]
        w_r = s.wei_v.at[pl.ds(2 * WIDTH, WIDTH)]
        w_n1 = s.wni_v.at[pl.ds(0, WIDTH)]
        w_n2 = s.wni_v.at[pl.ds(WIDTH, WIDTH)]
        own = s.look.at[pl.ds(0, NODES)]

        for name in SMALL:
            getattr(load, name).wait()

        def one(mask):
            return jnp.where(mask, 1.0, 0.0).astype(bf16)

        send_ids = jnp.concatenate([given.sendid[0:1, :], given.sendid[1:2, :]], axis=1)
        send_t = one(lax.broadcasted_iota(jnp.int32, (NODES, 2 * SLOTS), 0) == send_ids)
        for j in range(EDGES // 128):
            lanes = pl.ds(128 * j, 128)
            snd, rcv = given.sndid[j : j + 1, :], given.rcvid[j : j + 1, :]
            s.pick_t[pl.ds(0, NODES), lanes] = one(lax.broadcasted_iota(jnp.int32, (NODES, 128), 0) == rcv)
            s.pick_t[pl.ds(NODES, PICKS - NODES), lanes] = one(
                lax.broadcasted_iota(jnp.int32, (PICKS - NODES, 128), 0) == snd
            )
            snd_c = jnp.broadcast_to(snd, (128, 128)).T
            rcv_c = jnp.broadcast_to(rcv, (128, 128)).T
            lane = lax.broadcasted_iota(jnp.int32, (128, 128), 1)
            for i in range(2):
                s.pick[pl.ds(128 * j, 128), pl.ds(128 * i, 128)] = one(rcv_c == lane + 128 * i)
            for i in range(3):
                s.pick[pl.ds(128 * j, 128), pl.ds(NODES + 128 * i, 128)] = one(snd_c == lane + 128 * i)
        s.proj[pl.ds(NODES + LOOKUP, 64)] = jnp.zeros((64, WIDTH), bf16)

        load.nodes.wait()
        s.outgoing[...] = dot_tn(send_t, own[...]).astype(bf16)
        halo = [
            send(s.outgoing.at[pl.ds(0, SLOTS)], s.look.at[pl.ds(NODES + SLOTS, SLOTS)], s.hs.at[0], s.hq.at[0], beside(-1)),
            send(s.outgoing.at[pl.ds(SLOTS, SLOTS)], s.look.at[pl.ds(NODES, SLOTS)], s.hs.at[1], s.hq.at[1], beside(1)),
        ]
        barrier_wait()
        for copy in halo:
            copy.start()

        def tiles(body):
            chunks(EDGES, TILE, body)

        load.we.wait()
        load.edges.wait()

        def first(i):
            rows = pl.ds(i, TILE)
            s.pre[rows] = dot(s.edges_v[rows], w_e[...]) + given.eshift[...]

        tiles(first)
        load.ws.wait()
        s.proj[pl.ds(0, NODES)] = dot(own[...], w_r[...]).astype(bf16)
        for copy in halo:
            copy.wait_recv()
        s.proj[pl.ds(NODES, LOOKUP)] = dot(s.look[...], w_s[...]).astype(bf16)
        load.weo.wait()
        s.agg[...] = jnp.zeros((NODES, WIDTH), f32)

        def forward(i):
            rows = pl.ds(i, TILE)
            preact = s.pre[rows] + dot(s.pick[rows], s.proj[...])
            hidden, dact = silu_parts(preact)
            s.dact[rows] = dact
            hidden = hidden.astype(bf16)
            s.hidden[rows] = hidden
            linear = dot(hidden, s.weo_v[...]) + given.eoff[...]
            normed, invstd = layer_norm(linear)
            s.normed[rows] = normed
            s.invstd[rows] = jnp.broadcast_to(invstd, (TILE, 128))
            fresh = (s.edges_v[rows].astype(f32) + given.egain[...] * normed).astype(bf16)
            s.agg[...] += dot(s.pick_t[pl.ds(0, NODES), pl.ds(i, TILE)], fresh)

        tiles(forward)
        load.wni.wait()
        agg = s.agg[...].astype(bf16)
        s.agg_b[...] = agg
        npre = dot(own[...], w_n1[...]) + dot(agg, w_n2[...]) + given.nshift[...]
        nhid, ndact = silu_parts(npre)
        nhid = nhid.astype(bf16)
        s.nhid[...] = nhid
        load.wno.wait()
        nlinear = dot(nhid, s.wno_v[...]) + given.noff[...]
        nnormed, ninvstd = layer_norm(nlinear)
        load.ncot.wait()
        cotan = s.ncot_v[...].astype(f32)
        lback = norm_back(cotan, nnormed, ninvstd, given.ngain[...])
        lhalf = lback.astype(bf16)
        s.lhalf[...] = lhalf
        pback = dot_nt(lhalf, s.wno_v[...]) * ndact
        phalf = pback.astype(bf16)
        s.phalf[...] = phalf
        s.back_b[...] = dot_nt(phalf, w_n2[...]).astype(bf16)
        for row, values in ((3, pback), (4, lback), (5, cotan * nnormed)):
            total = jnp.sum(column_sums(values), axis=0, keepdims=True) * node_norm
            bufs.vc[0, pl.ds(row, 1)] = total
        bufs.vc[0, pl.ds(6, 2)] = jnp.zeros((2, WIDTH), f32)
        for j in range(2):
            cols = pl.ds(256 * j, 256)
            flat[pl.ds(2048 + 256 * j, 256)] = dot_tn(s.look[pl.ds(0, NODES), cols], phalf) * node_norm
            flat[pl.ds(2560 + 256 * j, 256)] = dot_tn(s.agg_b[:, cols], phalf) * node_norm
            flat[pl.ds(3072 + 256 * j, 256)] = dot_tn(s.nhid[:, cols], lhalf) * node_norm
        red.round_blocks(0)
        red.core_start(0)
        s.sums[...] = jnp.zeros((3, 8, WIDTH), f32)
        load.ecot.wait()

        def upstream(rows):
            return s.ecot_v[rows].astype(f32) + dot(s.pick[rows, pl.ds(0, NODES)], s.back_b[...])

        def backward_one(i):
            rows = pl.ds(i, TILE)
            fresh_back = upstream(rows)
            s.pre[rows] = fresh_back
            normed = s.normed[rows]
            eback = norm_back(fresh_back, normed, s.invstd[rows, pl.ds(0, 1)], given.egain[...])
            s.elhalf[rows] = eback.astype(bf16)
            s.sums[1] += column_sums(eback)
            s.sums[2] += column_sums(fresh_back * normed)

        tiles(backward_one)
        red.first_start(0)

        def grow(left, right, row, scale, count=2):
            def body(j):
                cols = pl.ds(pl.multiple_of(j, 256), 256)
                flat[pl.ds(pl.multiple_of(row + j, 64), 256)] = dot_tn(left[:, cols], right[...]) * scale

            chunks(256 * count, 256, body)

        grow(s.hidden, s.elhalf, 1536, edge_norm)
        red.round_blocks(1)
        red.core_start(1)

        def backward_two(i):
            rows = pl.ds(i, TILE)
            epback = dot_nt(s.elhalf[rows], s.weo_v[...]) * s.dact[rows]
            s.ephalf[rows] = epback.astype(bf16)
            s.sums[0] += column_sums(epback)

        tiles(backward_two)
        for row in range(3):
            bufs.vc[0, pl.ds(row, 1)] = jnp.sum(s.sums[row], axis=0, keepdims=True) * edge_norm
        red.vector_start(0)
        red.first_start(1)
        grow(s.edges_v, s.ephalf, 0, edge_norm)

        def gather(i):
            rows = pl.ds(i, 128)
            s.gathered[rows] = dot(s.pick_t[rows], s.ephalf[...]).astype(bf16)

        chunks(PICKS, 128, gather)
        r_rows, s_rows = pl.ds(0, NODES), pl.ds(NODES, LOOKUP)
        grow(s.look, s.gathered.at[s_rows], 512, edge_norm)
        grow(s.look.at[r_rows], s.gathered.at[r_rows], 1024, edge_norm)
        red.round_blocks(2)
        red.core_start(2)
        s.rim[...] = dot_nt(s.gathered[pl.ds(2 * NODES, 2 * SLOTS)], w_s[...]).astype(bf16)
        rims = [
            send(s.rim.at[pl.ds(0, SLOTS)], s.back.at[pl.ds(SLOTS, SLOTS)], s.hs.at[2], s.hq.at[2], beside(-1)),
            send(s.rim.at[pl.ds(SLOTS, SLOTS)], s.back.at[pl.ds(0, SLOTS)], s.hs.at[3], s.hq.at[3], beside(1)),
        ]
        for copy in rims:
            copy.start()
        red.vector_start(1, red.vector_value(0))
        red.second_y_start(0)

        def edge_grads(i):
            rows = pl.ds(i, TILE)
            ge_out[rows] = (s.pre[rows] + dot_nt(s.ephalf[rows], w_e[...])).astype(bf16)

        edge_grads(0)
        red.first_start(2)
        red.second_y_start(1)
        red.vector_start(2, red.vector_value(1))
        edge_grads(TILE)
        s.gnodes[...] = (
            s.ncot_v[...].astype(f32)
            + dot_nt(s.phalf[...], w_n1[...])
            + dot_nt(s.gathered[r_rows], w_r[...])
            + dot_nt(s.gathered[pl.ds(NODES, NODES)], w_s[...])
        )
        for copy in rims:
            copy.wait_recv()
        gn_out[...] = s.gnodes[...] + dot(send_t, s.back[...])
        red.second_y_start(2)
        red.second_x_start()
        red.vector_start(3, red.vector_value(2))
        red.third_start()
        sums = red.vector_value(3)
        for j in range(WIDTH // 128):
            v_out[pl.ds(j, 6, stride=WIDTH // 128), :] = sums[0:6, 128 * j : 128 * j + 128]
        red.finish(w_out)
        red.drain()
        red.vector_drain()
        for copy in halo + rims:
            copy.wait_send()

    hbm_spec = pl.BlockSpec(memory_space=pltpu.HBM)
    vmem_spec = pl.BlockSpec(memory_space=pltpu.VMEM)
    return pl.pallas_call(
        kernel,
        out_shape=(
            jax.ShapeDtypeStruct((NODES, WIDTH), jnp.float32),
            jax.ShapeDtypeStruct((EDGES, WIDTH), jnp.bfloat16),
            jax.ShapeDtypeStruct((SHARE * WIDTH // 128, 128), jnp.float32),
            jax.ShapeDtypeStruct((6 * WIDTH // 128, 128), jnp.float32),
        ),
        in_specs=[hbm_spec] * 17,
        out_specs=(vmem_spec, vmem_spec, vmem_spec, vmem_spec),
        scratch_shapes=[*compute_scratch().values(), *reduce_scratch().values()],
        compiler_params=pltpu.CompilerParams(
            collective_id=0, has_side_effects=True, vmem_limit_bytes=60 * 1024 * 1024
        ),
        name="layer_back",
    )(*operands)


def store(*values):
    count = len(values)

    def kernel(*refs):
        sems = refs[2 * count]
        copies = [pltpu.make_async_copy(refs[i], refs[count + i], sems.at[i]) for i in range(count)]
        for copy in copies:
            copy.start()
        for copy in copies:
            copy.wait()

    return pl.pallas_call(
        kernel,
        out_shape=tuple(jax.ShapeDtypeStruct(value.shape, value.dtype) for value in values),
        in_specs=[pl.BlockSpec(memory_space=pltpu.VMEM)] * count,
        out_specs=(pl.BlockSpec(memory_space=pltpu.HBM),) * count,
        scratch_shapes=[pltpu.SemaphoreType.DMA((count,))],
        name="store",
    )(*values)


def per_device(
    nodes,
    edges,
    node_cotan,
    edge_cotan,
    edge_inner,
    edge_outer,
    node_inner,
    node_outer,
    edge_shift,
    edge_offset,
    edge_gain,
    node_shift,
    node_offset,
    node_gain,
    send_rows,
    senders,
    receivers,
):
    devices_all = lax.axis_size("region") * lax.axis_size("patch")
    edge_norm = 1.0 / math.sqrt(EDGES * devices_all)
    node_norm = 1.0 / math.sqrt(NODES * devices_all)
    vectors = (edge_shift, edge_offset, edge_gain, node_shift, node_offset, node_gain)
    grad_nodes, grad_edges, weights, vector_sums = layer(
        edge_norm,
        node_norm,
        nodes,
        edges,
        node_cotan,
        edge_cotan,
        edge_inner,
        edge_outer,
        node_inner,
        node_outer,
        *(vector.reshape(1, WIDTH) for vector in vectors),
        send_rows.reshape(2, SLOTS),
        senders.reshape(EDGES // 128, 128),
        receivers.reshape(EDGES // 128, 128),
    )
    grad_nodes, grad_edges, weights, vector_sums = store(grad_nodes, grad_edges, weights, vector_sums)
    return (grad_nodes, grad_edges, weights.reshape(-1), vector_sums.reshape(-1))


def solution(mesh):
    in_specs = (
        P(("region", "patch"), None),
        P(("region", "patch"), None),
        P(("region", "patch"), None),
        P(("region", "patch"), None),
        P(),
        P(),
        P(),
        P(),
        P(),
        P(),
        P(),
        P(),
        P(),
        P(),
        P("region", "patch", None, None),
        P(("region", "patch")),
        P(("region", "patch")),
    )
    out_specs = (
        P(("region", "patch"), None),
        P(("region", "patch"), None),
        P(("region", "patch")),
        P(),
    )
    return jax.shard_map(
        per_device, mesh=mesh, in_specs=in_specs, out_specs=out_specs, check_vma=False
    )
```

time: 99.2 us -> 59.4 us (0.60)
  the two profiles are of different devices: /device:TPU:1 before, /device:TPU:2 now
where the time goes in v2:
time: 59.4 us; the launch traced here: 58.6 us
  Pallas kernels  57.9 us (97%)
  between operations  0.65 us (1%)
    pallas_call x1, Pallas kernels, layer(): pl.pallas_call(kernel, out_shape=(jax.ShapeDtypeStruct((NODES, WIDTH), jn...  55.4 us
    pallas_call x1, Pallas kernels, store(): pl.pallas_call(kernel, out_shape=tuple((jax.ShapeDtypeStruct(value.shape,...  2.54 us

profile of v2, /device:TPU:2, one launch (start us, length us, event | category | flops | bytes accessed | tf_op | source)
XLA Modules:
  0.0 58.6 jit_solution(13932200012294604191)
XLA Ops:
  0.6 55.4 %layer_back.1 = (f32[256,512]{1,0:T(8,128)}, bf16[1024,512]{1,0:T(8,128)(2,1)}, f32[56,128]{1,0:T(8,128)}, f32[24,128]{1,0:T(8,128)}) custom-call(bf16[256,512]{1,0:T(8,128)(2,1)} %refs_0_.1, bf16[1024,512]{1,0:T(8,128)(2,1)} %refs_1_.1, bf16[256,512]{1,0:T(8,128)(2,1)} %refs_2_.1, bf16[1024,512]{1,0:T(8,128)(2,1)} %refs_3_.1, bf16[1536,512]{1,0:T(8,128)(2,1)} %refs_4_.1, ...), custom_call_target="tpu_custom_call" | custom-call | tf_op jit(solution)/shard_map/layer_back/pallas_call | solution.py:687
  56.0 2.5 %store.1 = (f32[256,512]{1,0:T(8,128)}, bf16[1024,512]{1,0:T(8,128)(2,1)}, f32[56,128]{1,0:T(8,128)}, f32[24,128]{1,0:T(8,128)}) custom-call(f32[256,512]{1,0:T(8,128)} %get-tuple-element.12.refs_0_, bf16[1024,512]{1,0:T(8,128)(2,1)} %get-tuple-element.13.refs_1_, f32[56,128]{1,0:T(8,128)} %get-tuple-element.14.refs_2_, f32[24,128]{1,0:T(8,128)} %get-tuple-element.15.refs_3_), custom_call_target="tpu_custom_call" | custom-call | tf_op jit(solution)/shard_map/store/pallas_call | solution.py:716

commit v3 on v2

--- a/solution.py
+++ b/solution.py
@@ -10,7 +10,7 @@
 
 MESH = pl.DeviceIdType.MESH
 NX, NC, NY, NZ = 4, 2, 4, 8
-WIDTH, HALF = 512, 256
+WIDTH, XW, YW = 512, 128, 384
 BLOCK, QUARTER, SHARE, PAD = 448, 112, 14, 16
 
 
@@ -58,6 +58,11 @@
     )
 
 
+def waiter(ref, sem):
+    x, c, y, z = coordinates()
+    return send(ref, ref, sem, sem, at(x, 1 - c, y, z))
+
+
 def chunks(total, step, body):
     def one(i, carry):
         body(pl.multiple_of(i * step, step))
@@ -73,35 +78,30 @@
         sb=pltpu.VMEM((NX, NC, BLOCK, WIDTH), bf16),
         r0=pltpu.VMEM((NX, BLOCK, WIDTH), bf16),
         b1=pltpu.VMEM((NX, BLOCK, WIDTH), bf16),
-        r1x=pltpu.VMEM((NX, BLOCK, HALF), bf16),
-        r1y=pltpu.VMEM((NY, NX, QUARTER, HALF), bf16),
-        a1x=pltpu.VMEM((NY, QUARTER, HALF), f32),
-        b2x=pltpu.VMEM((NY, QUARTER, HALF), bf16),
-        r2x=pltpu.VMEM((NY, QUARTER, HALF), bf16),
-        a1y=pltpu.VMEM((NX, QUARTER, HALF), f32),
-        b2y=pltpu.VMEM((NX, QUARTER, HALF), bf16),
-        r2y=pltpu.VMEM((NX, QUARTER, HALF), bf16),
-        packed=pltpu.VMEM((NZ, PAD, WIDTH), f32),
-        b3=pltpu.VMEM((NZ, PAD, WIDTH), bf16),
-        r3=pltpu.VMEM((NZ, PAD, WIDTH), bf16),
-        s0=dma((NX,)),
+        r1x=pltpu.VMEM((NX, BLOCK, XW), bf16),
+        r1y=pltpu.VMEM((NY, NX, QUARTER, YW), bf16),
+        a1x=pltpu.VMEM((NY, QUARTER, XW), f32),
+        b2x=pltpu.VMEM((NY, QUARTER, XW), bf16),
+        r2x=pltpu.VMEM((NY, QUARTER, XW), bf16),
+        a1y=pltpu.VMEM((NX, QUARTER, YW), f32),
+        b2y=pltpu.VMEM((NX, QUARTER, YW), bf16),
+        r2y=pltpu.VMEM((NX, QUARTER, YW), bf16),
+        packed=pltpu.VMEM((NZ, PAD, XW + YW), f32),
+        b3=pltpu.VMEM((NZ, PAD, XW + YW), bf16),
+        r3=pltpu.VMEM((NZ, PAD, XW + YW), bf16),
+        sent=dma((6,)),
         q0=dma((NX,)),
-        s1x=dma((NX,)),
-        q1x=dma((NX,)),
-        s1y=dma((3, NY)),
-        q1y=dma((3, NY)),
-        s2x=dma((NY,)),
-        q2x=dma((NY,)),
-        s2y=dma((NX,)),
-        q2y=dma((NX,)),
-        s3=dma((NZ,)),
-        q3=dma((NZ,)),
+        q1x=dma,
+        q1y=dma((NX,)),
+        q2x=dma,
+        q2y=dma,
+        q3=dma,
         vc=pltpu.VMEM((2, 8, WIDTH), f32),
         vx=pltpu.VMEM((NX, 8, WIDTH), f32),
         vy=pltpu.VMEM((NY, 8, WIDTH), f32),
         vz=pltpu.VMEM((NZ, 8, WIDTH), f32),
-        us=dma((1 + NX + NY + NZ,)),
-        uq=dma((1 + NX + NY + NZ,)),
+        us=dma((4,)),
+        uq=dma((4,)),
     )
 
 
@@ -109,7 +109,7 @@
     def __init__(self, g, bufs):
         self.g, self.b = g, bufs
         self.x, self.c, self.y, self.z = coordinates()
-        self.piece_xs = ((3,), (2,), (0, 1))
+        self.piece_xs = ((3,), (2,), (0,), (1,))
 
     def core_copies(self, piece):
         b = self.b
@@ -117,7 +117,7 @@
             send(
                 b.sb.at[xx, 1 - self.c],
                 b.r0.at[xx],
-                b.s0.at[xx],
+                b.sent.at[0],
                 b.q0.at[xx],
                 at(self.x, 1 - self.c, self.y, self.z),
             )
@@ -131,20 +131,19 @@
     def round_blocks(self, piece):
         b, g = self.b, self.g
         for xx in self.piece_xs[piece]:
-            for cc in range(NC):
-
-                def body(i, xx=xx, cc=cc):
-                    b.sb[xx, cc, pl.ds(i, 64)] = g[xx, cc, pl.ds(i, 64)].astype(jnp.bfloat16)
-
-                chunks(BLOCK, 64, body)
+
+            def body(i, xx=xx):
+                b.sb[xx, 1 - self.c, pl.ds(i, 64)] = g[xx, 1 - self.c, pl.ds(i, 64)].astype(jnp.bfloat16)
+
+            chunks(BLOCK, 64, body)
 
     def first_x(self, xx):
         b = self.b
         return send(
-            b.b1.at[xx, :, pl.ds(0, HALF)],
+            b.b1.at[xx, :, pl.ds(0, XW)],
             b.r1x.at[self.x],
-            b.s1x.at[xx],
-            b.q1x.at[self.x],
+            b.sent.at[1],
+            b.q1x,
             at(xx, self.c, self.y, self.z),
         )
 
@@ -154,10 +153,10 @@
         xs = self.piece_xs[piece]
         blocks = pl.ds(xs[0], len(xs))
         return send(
-            b.b1.at[blocks, pl.ds(pl.multiple_of(to * QUARTER, 16), QUARTER), pl.ds(HALF, HALF)],
+            b.b1.at[blocks, pl.ds(pl.multiple_of(to * QUARTER, 16), QUARTER), pl.ds(XW, YW)],
             b.r1y.at[k, blocks],
-            b.s1y.at[piece, k],
-            b.q1y.at[piece, k],
+            b.sent.at[2],
+            b.q1y.at[xs[0]],
             at(self.x, self.c, to, self.z),
         )
 
@@ -187,8 +186,8 @@
         return send(
             b.b2x.at[to],
             b.r2x.at[k],
-            b.s2x.at[k],
-            b.q2x.at[k],
+            b.sent.at[3],
+            b.q2x,
             at(self.x, self.c, to, self.z),
         )
 
@@ -197,20 +196,20 @@
         return send(
             b.b2y.at[xx],
             b.r2y.at[self.x],
-            b.s2y.at[xx],
-            b.q2y.at[self.x],
+            b.sent.at[4],
+            b.q2y,
             at(xx, self.c, self.y, self.z),
         )
 
     def second_y_start(self, piece):
         b, g = self.b, self.g
-        for k in (1, 3, 2):
-            self.first_y(piece, k).wait_recv()
+        for xx in self.piece_xs[piece]:
+            waiter(b.r1y.at[pl.ds(1, NY - 1), xx], b.q1y.at[xx]).wait_recv()
         base = self.y * QUARTER
         for xx in self.piece_xs[piece]:
 
             def body(i, xx=xx):
-                total = g[xx, self.c, pl.ds(pl.multiple_of(base + i, 16), 16), pl.ds(HALF, HALF)]
+                total = g[xx, self.c, pl.ds(pl.multiple_of(base + i, 16), 16), pl.ds(XW, YW)]
                 for k in range(1, NY):
                     total += b.r1y[k, xx, pl.ds(i, 16)].astype(jnp.float32)
                 b.a1y[xx, pl.ds(i, 16)] = total
@@ -223,21 +222,13 @@
             def _(xx=xx):
                 self.second_y(xx).start()
 
-    def from_x(self, recv, sems, like):
-        found = []
-        for k in (1, 3, 2):
-            source = lax.rem(self.x + k, NX)
-            found.append(send(like, recv.at[source], sems[0].at[source], sems[1].at[source], at(source, self.c, self.y, self.z)))
-        return found
-
     def second_x_start(self):
         b, g = self.b, self.g
-        for copy in self.from_x(b.r1x, (b.s1x, b.q1x), b.r1x.at[0]):
-            copy.wait_recv()
+        waiter(b.r1x.at[pl.ds(0, NX - 1)], b.q1x).wait_recv()
         for yy in range(NY):
 
             def body(i, yy=yy):
-                total = g[self.x, self.c, pl.ds(yy * QUARTER + i, 16), pl.ds(0, HALF)]
+                total = g[self.x, self.c, pl.ds(yy * QUARTER + i, 16), pl.ds(0, XW)]
                 for k in range(1, NX):
                     source = lax.rem(self.x + k, NX)
                     total += b.r1x[source, pl.ds(yy * QUARTER + i, 16)].astype(jnp.float32)
@@ -254,17 +245,15 @@
         return send(
             b.b3.at[to],
             b.r3.at[k],
-            b.s3.at[k],
-            b.q3.at[k],
+            b.sent.at[5],
+            b.q3,
             at(self.x, self.c, self.y, to),
         )
 
     def third_start(self):
         b = self.b
-        for k in range(1, NY):
-            self.second_x(k).wait_recv()
-        for copy in self.from_x(b.r2y, (b.s2y, b.q2y), b.r2y.at[0]):
-            copy.wait_recv()
+        waiter(b.r2x.at[pl.ds(1, NY - 1)], b.q2x).wait_recv()
+        waiter(b.r2y.at[pl.ds(0, NX - 1)], b.q2y).wait_recv()
         for i in range(NZ):
             rows = pl.ds(i * SHARE, SHARE)
             left = b.a1x[self.y, rows]
@@ -280,51 +269,46 @@
 
     def finish(self, out):
         b = self.b
-        for k in range(1, NZ):
-            self.third(k).wait_recv()
+        waiter(b.r3.at[pl.ds(1, NZ - 1)], b.q3).wait_recv()
         total = b.packed[self.z, pl.ds(0, SHARE)]
         for k in range(1, NZ):
             total += b.r3[k, pl.ds(0, SHARE)].astype(jnp.float32)
         for j in range(WIDTH // 128):
-            out[pl.ds(j, SHARE, stride=WIDTH // 128), :] = total[:, 128 * j : 128 * j + 128]
+            out[pl.ds(j, SHARE, stride=4), :] = total[:, 128 * j : 128 * j + 128]
 
     def drain(self):
-        for piece in range(len(self.piece_xs)):
-            for copy in self.core_copies(piece):
-                copy.wait_send()
-            for k in range(1, NY):
-                self.first_y(piece, k).wait_send()
-        for xx in range(NX):
-
-            @pl.when(self.x != xx)
-            def _(xx=xx):
-                self.first_x(xx).wait_send()
-                self.second_y(xx).wait_send()
-
-        for k in range(1, NY):
-            self.second_x(k).wait_send()
-        for k in range(1, NZ):
-            self.third(k).wait_send()
+        b = self.b
+        for i, ref in enumerate(
+            (
+                b.r0,
+                b.r1x.at[pl.ds(0, NX - 1)],
+                b.r1y.at[pl.ds(1, NY - 1)],
+                b.r2x.at[pl.ds(1, NY - 1)],
+                b.r2y.at[pl.ds(0, NX - 1)],
+                b.r3.at[pl.ds(1, NZ - 1)],
+            )
+        ):
+            waiter(ref, b.sent.at[i]).wait_send()
 
     def vector_copies(self, stage):
         b = self.b
         x, c, y, z = self.x, self.c, self.y, self.z
         if stage == 0:
             return [send(b.vc.at[0], b.vc.at[1], b.us.at[0], b.uq.at[0], at(x, 1 - c, y, z))]
-        buf, base, count, me = (
-            (b.vx, 1, NX, x),
-            (b.vy, 1 + NX, NY, y),
-            (b.vz, 1 + NX + NY, NZ, z),
-        )[stage - 1]
+        buf, count, me = ((b.vx, NX, x), (b.vy, NY, y), (b.vz, NZ, z))[stage - 1]
         found = []
         for k in range(1, count):
             to = lax.rem(me + k, count)
             device = (at(to, c, y, z), at(x, c, to, z), at(x, c, y, to))[stage - 1]
-            found.append((k, to, device, buf, base, me, count))
-        return [
-            send(buf.at[me], buf.at[me], b.us.at[base + k], b.uq.at[base + k], device)
-            for k, to, device, buf, base, me, count in found
-        ]
+            found.append(send(buf.at[me], buf.at[me], b.us.at[stage], b.uq.at[stage], device))
+        return found
+
+    def vector_bytes(self, stage):
+        b = self.b
+        if stage == 0:
+            return b.vc.at[1]
+        buf, count = ((b.vx, NX), (b.vy, NY), (b.vz, NZ))[stage - 1]
+        return buf.at[pl.ds(0, count - 1)]
 
     def vector_start(self, stage, value=None):
         b = self.b
@@ -335,8 +319,7 @@
 
     def vector_value(self, stage):
         b = self.b
-        for copy in self.vector_copies(stage):
-            copy.wait_recv()
+        waiter(self.vector_bytes(stage), b.uq.at[stage]).wait_recv()
         if stage == 0:
             return b.vc[0] + b.vc[1]
         buf = (b.vx, b.vy, b.vz)[stage - 1]
@@ -347,8 +330,7 @@
 
     def vector_drain(self):
         for stage in range(4):
-            for copy in self.vector_copies(stage):
-                copy.wait_send()
+            waiter(self.vector_bytes(stage), self.b.us.at[stage]).wait_send()
 
 
 NODES, EDGES, SLOTS, LOOKUP, PICKS = 256, 1024, 32, 320, 640
@@ -384,7 +366,8 @@
 
 def silu_parts(preact):
     sigmoid = 1.0 / (1.0 + jnp.exp(-preact))
-    return preact * sigmoid, sigmoid * (1.0 + preact * (1.0 - sigmoid))
+    hidden = preact * sigmoid
+    return hidden, sigmoid + hidden * (1.0 - sigmoid)
 
 
 def column_sums(values):
@@ -498,6 +481,18 @@
 
         send_ids = jnp.concatenate([given.sendid[0:1, :], given.sendid[1:2, :]], axis=1)
         send_t = one(lax.broadcasted_iota(jnp.int32, (NODES, 2 * SLOTS), 0) == send_ids)
+        s.proj[pl.ds(NODES + LOOKUP, 64)] = jnp.zeros((64, WIDTH), bf16)
+
+        load.nodes.wait()
+        s.outgoing[...] = dot_tn(send_t, own[...]).astype(bf16)
+        halo = [
+            send(s.outgoing.at[pl.ds(0, SLOTS)], s.look.at[pl.ds(NODES + SLOTS, SLOTS)], s.hs.at[0], s.hq.at[0], beside(-1)),
+            send(s.outgoing.at[pl.ds(SLOTS, SLOTS)], s.look.at[pl.ds(NODES, SLOTS)], s.hs.at[1], s.hq.at[1], beside(1)),
+        ]
+        barrier_wait()
+        for copy in halo:
+            copy.start()
+
         for j in range(EDGES // 128):
             lanes = pl.ds(128 * j, 128)
             snd, rcv = given.sndid[j : j + 1, :], given.rcvid[j : j + 1, :]
@@ -512,18 +507,6 @@
                 s.pick[pl.ds(128 * j, 128), pl.ds(128 * i, 128)] = one(rcv_c == lane + 128 * i)
             for i in range(3):
                 s.pick[pl.ds(128 * j, 128), pl.ds(NODES + 128 * i, 128)] = one(snd_c == lane + 128 * i)
-        s.proj[pl.ds(NODES + LOOKUP, 64)] = jnp.zeros((64, WIDTH), bf16)
-
-        load.nodes.wait()
-        s.outgoing[...] = dot_tn(send_t, own[...]).astype(bf16)
-        halo = [
-            send(s.outgoing.at[pl.ds(0, SLOTS)], s.look.at[pl.ds(NODES + SLOTS, SLOTS)], s.hs.at[0], s.hq.at[0], beside(-1)),
-            send(s.outgoing.at[pl.ds(SLOTS, SLOTS)], s.look.at[pl.ds(NODES, SLOTS)], s.hs.at[1], s.hq.at[1], beside(1)),
-        ]
-        barrier_wait()
-        for copy in halo:
-            copy.start()
-
         def tiles(body):
             chunks(EDGES, TILE, body)
 
@@ -581,13 +564,6 @@
             total = jnp.sum(column_sums(values), axis=0, keepdims=True) * node_norm
             bufs.vc[0, pl.ds(row, 1)] = total
         bufs.vc[0, pl.ds(6, 2)] = jnp.zeros((2, WIDTH), f32)
-        for j in range(2):
-            cols = pl.ds(256 * j, 256)
-            flat[pl.ds(2048 + 256 * j, 256)] = dot_tn(s.look[pl.ds(0, NODES), cols], phalf) * node_norm
-            flat[pl.ds(2560 + 256 * j, 256)] = dot_tn(s.agg_b[:, cols], phalf) * node_norm
-            flat[pl.ds(3072 + 256 * j, 256)] = dot_tn(s.nhid[:, cols], lhalf) * node_norm
-        red.round_blocks(0)
-        red.core_start(0)
         s.sums[...] = jnp.zeros((3, 8, WIDTH), f32)
         load.ecot.wait()
 
@@ -603,9 +579,15 @@
             s.elhalf[rows] = eback.astype(bf16)
             s.sums[1] += column_sums(eback)
             s.sums[2] += column_sums(fresh_back * normed)
+            j = i // TILE * 256
+            cols = pl.ds(j if isinstance(j, int) else pl.multiple_of(j, 256), 256)
+            flat[pl.ds(2048 + j, 256)] = dot_tn(s.look[pl.ds(0, NODES), cols], s.phalf[...]) * node_norm
+            flat[pl.ds(2560 + j, 256)] = dot_tn(s.agg_b[:, cols], s.phalf[...]) * node_norm
+            flat[pl.ds(3072 + j, 256)] = dot_tn(s.nhid[:, cols], s.lhalf[...]) * node_norm
 
         tiles(backward_one)
-        red.first_start(0)
+        red.round_blocks(0)
+        red.core_start(0)
 
         def grow(left, right, row, scale, count=2):
             def body(j):
@@ -615,6 +597,7 @@
             chunks(256 * count, 256, body)
 
         grow(s.hidden, s.elhalf, 1536, edge_norm)
+        red.first_start(0)
         red.round_blocks(1)
         red.core_start(1)
 
@@ -631,16 +614,15 @@
         red.first_start(1)
         grow(s.edges_v, s.ephalf, 0, edge_norm)
 
-        def gather(i):
-            rows = pl.ds(i, 128)
-            s.gathered[rows] = dot(s.pick_t[rows], s.ephalf[...]).astype(bf16)
-
-        chunks(PICKS, 128, gather)
+        live = pl.ds(0, NODES + LOOKUP)
+        s.gathered[live] = dot(s.pick_t[live], s.ephalf[...]).astype(bf16)
         r_rows, s_rows = pl.ds(0, NODES), pl.ds(NODES, LOOKUP)
         grow(s.look, s.gathered.at[s_rows], 512, edge_norm)
-        grow(s.look.at[r_rows], s.gathered.at[r_rows], 1024, edge_norm)
         red.round_blocks(2)
         red.core_start(2)
+        grow(s.look.at[r_rows], s.gathered.at[r_rows], 1024, edge_norm)
+        red.round_blocks(3)
+        red.core_start(3)
         s.rim[...] = dot_nt(s.gathered[pl.ds(2 * NODES, 2 * SLOTS)], w_s[...]).astype(bf16)
         rims = [
             send(s.rim.at[pl.ds(0, SLOTS)], s.back.at[pl.ds(SLOTS, SLOTS)], s.hs.at[2], s.hq.at[2], beside(-1)),
@@ -649,16 +631,17 @@
         for copy in rims:
             copy.start()
         red.vector_start(1, red.vector_value(0))
-        red.second_y_start(0)
 
         def edge_grads(i):
             rows = pl.ds(i, TILE)
             ge_out[rows] = (s.pre[rows] + dot_nt(s.ephalf[rows], w_e[...])).astype(bf16)
 
+        red.first_start(2)
+        red.first_start(3)
+        red.vector_start(2, red.vector_value(1))
+        for piece in range(2):
+            red.second_y_start(piece)
         edge_grads(0)
-        red.first_start(2)
-        red.second_y_start(1)
-        red.vector_start(2, red.vector_value(1))
         edge_grads(TILE)
         s.gnodes[...] = (
             s.ncot_v[...].astype(f32)
@@ -670,6 +653,7 @@
             copy.wait_recv()
         gn_out[...] = s.gnodes[...] + dot(send_t, s.back[...])
         red.second_y_start(2)
+        red.second_y_start(3)
         red.second_x_start()
         red.vector_start(3, red.vector_value(2))
         red.third_start()

time: 59.4 us -> 55.7 us (0.938); the launches traced: 58.6 us -> 55.6 us
  Pallas kernels: 57.9 us -> 55 us
    pallas_call x1, Pallas kernels: 55.4 us -> 52.4 us  [layer(): pl.pallas_call(kernel, out_shape=(jax.ShapeDtypeStruct((NODES, WIDTH), jn...]
where the time goes in v3:
time: 55.7 us; the launch traced here: 55.6 us
  Pallas kernels  55 us (99%)
  between operations  0.65 us (1%)
    pallas_call x1, Pallas kernels, layer(): pl.pallas_call(kernel, out_shape=(jax.ShapeDtypeStruct((NODES, WIDTH), jn...  52.4 us
    pallas_call x1, Pallas kernels, store(): pl.pallas_call(kernel, out_shape=tuple((jax.ShapeDtypeStruct(value.shape,...  2.54 us

profile of v3, /device:TPU:2, one launch (start us, length us, event | category | flops | bytes accessed | tf_op | source)
XLA Modules:
  0.0 55.6 jit_solution(16983014968513889533)
XLA Ops:
  0.6 52.4 %layer_back.1 = (f32[256,512]{1,0:T(8,128)}, bf16[1024,512]{1,0:T(8,128)(2,1)}, f32[56,128]{1,0:T(8,128)}, f32[24,128]{1,0:T(8,128)}) custom-call(bf16[256,512]{1,0:T(8,128)(2,1)} %refs_0_.1, bf16[1024,512]{1,0:T(8,128)(2,1)} %refs_1_.1, bf16[256,512]{1,0:T(8,128)(2,1)} %refs_2_.1, bf16[1024,512]{1,0:T(8,128)(2,1)} %refs_3_.1, bf16[1536,512]{1,0:T(8,128)(2,1)} %refs_4_.1, ...), custom_call_target="tpu_custom_call" | custom-call | tf_op jit(solution)/shard_map/layer_back/pallas_call | solution.py:671
  53.1 2.5 %store.1 = (f32[256,512]{1,0:T(8,128)}, bf16[1024,512]{1,0:T(8,128)(2,1)}, f32[56,128]{1,0:T(8,128)}, f32[24,128]{1,0:T(8,128)}) custom-call(f32[256,512]{1,0:T(8,128)} %get-tuple-element.12.refs_0_, bf16[1024,512]{1,0:T(8,128)(2,1)} %get-tuple-element.13.refs_1_, f32[56,128]{1,0:T(8,128)} %get-tuple-element.14.refs_2_, f32[24,128]{1,0:T(8,128)} %get-tuple-element.15.refs_3_), custom_call_target="tpu_custom_call" | custom-call | tf_op jit(solution)/shard_map/store/pallas_call | solution.py:700

commit v4 on v3

--- a/solution.py
+++ b/solution.py
@@ -10,7 +10,7 @@
 
 MESH = pl.DeviceIdType.MESH
 NX, NC, NY, NZ = 4, 2, 4, 8
-WIDTH, XW, YW = 512, 128, 384
+WIDTH, XW, YW, ZW = 512, 128, 256, 128
 BLOCK, QUARTER, SHARE, PAD = 448, 112, 14, 16
 
 
@@ -89,13 +89,25 @@
         packed=pltpu.VMEM((NZ, PAD, XW + YW), f32),
         b3=pltpu.VMEM((NZ, PAD, XW + YW), bf16),
         r3=pltpu.VMEM((NZ, PAD, XW + YW), bf16),
-        sent=dma((6,)),
+        pz=pltpu.VMEM((NZ, NX, NY, PAD, ZW), f32),
+        bz=pltpu.VMEM((NZ, NX, NY, PAD, ZW), bf16),
+        rz=pltpu.VMEM((NZ, NX, NY, PAD, ZW), bf16),
+        az=pltpu.VMEM((NX, NY, PAD, ZW), f32),
+        bzx=pltpu.VMEM((NX, NY, PAD, ZW), bf16),
+        rzx=pltpu.VMEM((NX, NY, PAD, ZW), bf16),
+        azy=pltpu.VMEM((NY, PAD, ZW), f32),
+        bzy=pltpu.VMEM((NY, PAD, ZW), bf16),
+        rzy=pltpu.VMEM((NY, PAD, ZW), bf16),
+        sent=dma((9,)),
         q0=dma((NX,)),
         q1x=dma,
         q1y=dma((NX,)),
         q2x=dma,
         q2y=dma,
         q3=dma,
+        qz=dma((NX,)),
+        qzx=dma,
+        qzy=dma,
         vc=pltpu.VMEM((2, 8, WIDTH), f32),
         vx=pltpu.VMEM((NX, 8, WIDTH), f32),
         vy=pltpu.VMEM((NY, 8, WIDTH), f32),
@@ -179,6 +191,59 @@
             @pl.when(self.x != xx)
             def _(xx=xx):
                 self.first_x(xx).start()
+
+        for xx in self.piece_xs[piece]:
+
+            def group(i, xx=xx):
+                yy = i // QUARTER
+                part = g[xx, self.c, pl.ds(i, QUARTER), pl.ds(XW + YW, ZW)]
+                for zz in range(NZ):
+                    rows = part[zz * SHARE : zz * SHARE + SHARE]
+                    b.pz[zz, xx, yy, pl.ds(0, SHARE)] = rows
+                    b.bz[zz, xx, yy, pl.ds(0, SHARE)] = rows.astype(jnp.bfloat16)
+
+            chunks(BLOCK, QUARTER, group)
+            for k in (4, 3, 5, 2, 6, 1, 7):
+                self.first_z(xx, k).start()
+
+    def first_z(self, xx, k):
+        b = self.b
+        to = lax.rem(self.z + k, NZ)
+        return send(b.bz.at[to, xx], b.rz.at[k, xx], b.sent.at[6], b.qz.at[xx], at(self.x, self.c, self.y, to))
+
+    def second_z(self, xx):
+        b = self.b
+        return send(b.bzx.at[xx], b.rzx.at[self.x], b.sent.at[7], b.qzx, at(xx, self.c, self.y, self.z))
+
+    def second_z_start(self, piece):
+        b = self.b
+        for xx in self.piece_xs[piece]:
+            waiter(b.rz.at[pl.ds(1, NZ - 1), xx], b.qz.at[xx]).wait_recv()
+            total = b.pz[self.z, xx]
+            for k in range(1, NZ):
+                total += b.rz[k, xx].astype(jnp.float32)
+            b.az[xx] = total
+            b.bzx[xx] = total.astype(jnp.bfloat16)
+
+            @pl.when(self.x != xx)
+            def _(xx=xx):
+                self.second_z(xx).start()
+
+    def third_z(self, k):
+        b = self.b
+        to = lax.rem(self.y + k, NY)
+        return send(b.bzy.at[to], b.rzy.at[k], b.sent.at[8], b.qzy, at(self.x, self.c, to, self.z))
+
+    def third_z_start(self):
+        b = self.b
+        waiter(b.rzx.at[pl.ds(0, NX - 1)], b.qzx).wait_recv()
+        total = b.az[self.x]
+        for k in range(1, NX):
+            total += b.rzx[lax.rem(self.x + k, NX)].astype(jnp.float32)
+        b.azy[...] = total
+        b.bzy[...] = total.astype(jnp.bfloat16)
+        for k in (2, 1, 3):
+            self.third_z(k).start()
 
     def second_x(self, k):
         b = self.b
@@ -273,8 +338,13 @@
         total = b.packed[self.z, pl.ds(0, SHARE)]
         for k in range(1, NZ):
             total += b.r3[k, pl.ds(0, SHARE)].astype(jnp.float32)
-        for j in range(WIDTH // 128):
+        for j in range(3):
             out[pl.ds(j, SHARE, stride=4), :] = total[:, 128 * j : 128 * j + 128]
+        waiter(b.rzy.at[pl.ds(1, NY - 1)], b.qzy).wait_recv()
+        last = b.azy[self.y, pl.ds(0, SHARE)]
+        for k in range(1, NY):
+            last += b.rzy[k, pl.ds(0, SHARE)].astype(jnp.float32)
+        out[pl.ds(3, SHARE, stride=4), :] = last
 
     def drain(self):
         b = self.b
@@ -286,6 +356,9 @@
                 b.r2x.at[pl.ds(1, NY - 1)],
                 b.r2y.at[pl.ds(0, NX - 1)],
                 b.r3.at[pl.ds(1, NZ - 1)],
+                b.rz.at[pl.ds(1, NZ - 1)],
+                b.rzx.at[pl.ds(0, NX - 1)],
+                b.rzy.at[pl.ds(1, NY - 1)],
             )
         ):
             waiter(ref, b.sent.at[i]).wait_send()
@@ -641,6 +714,7 @@
         red.vector_start(2, red.vector_value(1))
         for piece in range(2):
             red.second_y_start(piece)
+            red.second_z_start(piece)
         edge_grads(0)
         edge_grads(TILE)
         s.gnodes[...] = (
@@ -653,8 +727,11 @@
             copy.wait_recv()
         gn_out[...] = s.gnodes[...] + dot(send_t, s.back[...])
         red.second_y_start(2)
+        red.second_z_start(2)
         red.second_y_start(3)
+        red.second_z_start(3)
         red.second_x_start()
+        red.third_z_start()
         red.vector_start(3, red.vector_value(2))
         red.third_start()
         sums = red.vector_value(3)

time: 55.7 us -> 53.6 us (0.962)
  Pallas kernels: 55 us -> 52.9 us
    pallas_call x1, Pallas kernels: 52.4 us -> 50.4 us  [layer(): pl.pallas_call(kernel, out_shape=(jax.ShapeDtypeStruct((NODES, WIDTH), jn...]
where the time goes in v4:
time: 53.6 us; the launch traced here: 53.5 us
  Pallas kernels  52.9 us (99%)
  between operations  0.65 us (1%)
    pallas_call x1, Pallas kernels, layer(): pl.pallas_call(kernel, out_shape=(jax.ShapeDtypeStruct((NODES, WIDTH), jn...  50.4 us
    pallas_call x1, Pallas kernels, store(): pl.pallas_call(kernel, out_shape=tuple((jax.ShapeDtypeStruct(value.shape,...  2.54 us

profile of v4, /device:TPU:2, one launch (start us, length us, event | category | flops | bytes accessed | tf_op | source)
XLA Modules:
  0.0 53.5 jit_solution(12405065948714242814)
XLA Ops:
  0.6 50.4 %layer_back.1 = (f32[256,512]{1,0:T(8,128)}, bf16[1024,512]{1,0:T(8,128)(2,1)}, f32[56,128]{1,0:T(8,128)}, f32[24,128]{1,0:T(8,128)}) custom-call(bf16[256,512]{1,0:T(8,128)(2,1)} %refs_0_.1, bf16[1024,512]{1,0:T(8,128)(2,1)} %refs_1_.1, bf16[256,512]{1,0:T(8,128)(2,1)} %refs_2_.1, bf16[1024,512]{1,0:T(8,128)(2,1)} %refs_3_.1, bf16[1536,512]{1,0:T(8,128)(2,1)} %refs_4_.1, ...), custom_call_target="tpu_custom_call" | custom-call | tf_op jit(solution)/shard_map/layer_back/pallas_call | solution.py:748
  51.0 2.5 %store.1 = (f32[256,512]{1,0:T(8,128)}, bf16[1024,512]{1,0:T(8,128)(2,1)}, f32[56,128]{1,0:T(8,128)}, f32[24,128]{1,0:T(8,128)}) custom-call(f32[256,512]{1,0:T(8,128)} %get-tuple-element.12.refs_0_, bf16[1024,512]{1,0:T(8,128)(2,1)} %get-tuple-element.13.refs_1_, f32[56,128]{1,0:T(8,128)} %get-tuple-element.14.refs_2_, f32[24,128]{1,0:T(8,128)} %get-tuple-element.15.refs_3_), custom_call_target="tpu_custom_call" | custom-call | tf_op jit(solution)/shard_map/store/pallas_call | solution.py:777

commit v5 on v4

--- a/solution.py
+++ b/solution.py
@@ -438,7 +438,7 @@
 
 
 def silu_parts(preact):
-    sigmoid = 1.0 / (1.0 + jnp.exp(-preact))
+    sigmoid = 0.5 * jnp.tanh(0.5 * preact) + 0.5
     hidden = preact * sigmoid
     return hidden, sigmoid + hidden * (1.0 - sigmoid)
 
@@ -581,7 +581,8 @@
             for i in range(3):
                 s.pick[pl.ds(128 * j, 128), pl.ds(NODES + 128 * i, 128)] = one(snd_c == lane + 128 * i)
         def tiles(body):
-            chunks(EDGES, TILE, body)
+            for i in range(0, EDGES, TILE):
+                body(i)
 
         load.we.wait()
         load.edges.wait()

time: 53.6 us -> 52.9 us (0.987)
  Pallas kernels: 52.9 us -> 52.1 us
    pallas_call x1, Pallas kernels: 50.4 us -> 49.6 us  [layer(): pl.pallas_call(kernel, out_shape=(jax.ShapeDtypeStruct((NODES, WIDTH), jn...]
where the time goes in v5:
time: 52.9 us; the launch traced here: 52.8 us
  Pallas kernels  52.1 us (98%)
  between operations  0.65 us (1%)
    pallas_call x1, Pallas kernels, layer(): pl.pallas_call(kernel, out_shape=(jax.ShapeDtypeStruct((NODES, WIDTH), jn...  49.6 us
    pallas_call x1, Pallas kernels, store(): pl.pallas_call(kernel, out_shape=tuple((jax.ShapeDtypeStruct(value.shape,...  2.54 us

profile of v5, /device:TPU:2, one launch (start us, length us, event | category | flops | bytes accessed | tf_op | source)
XLA Modules:
  0.0 52.8 jit_solution(6163431415575067488)
XLA Ops:
  0.6 49.6 %layer_back.1 = (f32[256,512]{1,0:T(8,128)}, bf16[1024,512]{1,0:T(8,128)(2,1)}, f32[56,128]{1,0:T(8,128)}, f32[24,128]{1,0:T(8,128)}) custom-call(bf16[256,512]{1,0:T(8,128)(2,1)} %refs_0_.1, bf16[1024,512]{1,0:T(8,128)(2,1)} %refs_1_.1, bf16[256,512]{1,0:T(8,128)(2,1)} %refs_2_.1, bf16[1024,512]{1,0:T(8,128)(2,1)} %refs_3_.1, bf16[1536,512]{1,0:T(8,128)(2,1)} %refs_4_.1, ...), custom_call_target="tpu_custom_call" | custom-call | tf_op jit(solution)/shard_map/layer_back/pallas_call | solution.py:749
  50.2 2.5 %store.1 = (f32[256,512]{1,0:T(8,128)}, bf16[1024,512]{1,0:T(8,128)(2,1)}, f32[56,128]{1,0:T(8,128)}, f32[24,128]{1,0:T(8,128)}) custom-call(f32[256,512]{1,0:T(8,128)} %get-tuple-element.12.refs_0_, bf16[1024,512]{1,0:T(8,128)(2,1)} %get-tuple-element.13.refs_1_, f32[56,128]{1,0:T(8,128)} %get-tuple-element.14.refs_2_, f32[24,128]{1,0:T(8,128)} %get-tuple-element.15.refs_3_), custom_call_target="tpu_custom_call" | custom-call | tf_op jit(solution)/shard_map/store/pallas_call | solution.py:778
